TPU v7x, 32 devices: a whole 2x2x4 slice. The times are simulated.
32 devices in a mesh: twin: 2 (over y), gx: 4 (over z), gy: 2 (over core), gz: 2 (over x).
Axes of the slice: x: 2, y: 2, z: 4, core: 2. Of those that a mesh axis runs over, the one named last changes fastest.
Arguments:
- potential: float32 [64, 32, 256], P(('twin', 'gx'), 'gy', 'gz'), parts along dimension 0, may hold values from 0 to 1
- gating: float32 [64, 32, 256], P(('twin', 'gx'), 'gy', 'gz'), parts along dimension 0, may hold values from 0 to 1
- adjoint_v: float32 [64, 32, 256], P(('twin', 'gx'), 'gy', 'gz'), parts along dimension 0, may hold values from -6 to 6
- adjoint_h: float32 [64, 32, 256], P(('twin', 'gx'), 'gy', 'gz'), parts along dimension 0, may hold values from -6 to 6
- recorded: float32 [64, 32, 256], P(('twin', 'gx'), 'gy', 'gz'), parts along dimension 0, may hold values from 0 to 1
- tissue_mask: int32 [64, 32, 256], P(('twin', 'gx'), 'gy', 'gz'), parts along dimension 0, may hold values from 0 to 1
- fibre_sector: int32 [64, 32, 256], P(('twin', 'gx'), 'gy', 'gz'), parts along dimension 0, may hold values from 0 to 11
- region_label: int32 [64, 32, 256], P(('twin', 'gx'), 'gy', 'gz'), parts along dimension 0, may hold values from 0 to 15
- fibre_table: float32 [24, 9], P('twin'), parts along dimension 0, may hold values from 0.005 to 0.025
- conductance: float32 [32], P('twin'), parts along dimension 0, may hold values from 0.5 to 2
Outputs:
- lambda_v: float32 [64, 32, 256], P(('twin', 'gx'), 'gy', 'gz'), parts along dimension 0
- lambda_h: float32 [64, 32, 256], P(('twin', 'gx'), 'gy', 'gz'), parts along dimension 0
- sensitivity: float32 [32], P('twin'), parts along dimension 0
There are 2 independent parts, one for each index of `twin`. A program takes and returns all parts, laid end to end along the dimension named above; each array names one. Nothing has to cross between parts.
All inputs are finite; a program needn't handle non-finite values.
Results may differ from a plain program's by a relative error of at most 0.0003.
Values sent between devices are 32-bit elements; how exact they have to be, the bound alone decides.
No kernel may reach another device: no remote copies, remote signals or barrier semaphores. Data moves between devices by JAX's collectives and lax.ppermute only.
A program may use at most 64 MiB of HBM per device.

v0:
```python
import math

import jax
import jax.numpy as jnp
from jax import lax
from jax.sharding import PartitionSpec as P

WINDOW_STEPS = 3


step_size = 0.1
tau_inward = 0.3
tau_outward = 6.0
tau_opening = 12.0
tau_closing = 15.0
gate_level = 0.13
gate_width = 0.02
gradient_gain = 30.0
PAIR_OFFSETS = (
    (1, 0, 0),
    (0, 1, 0),
    (0, 0, 1),
    (1, 1, 0),
    (1, -1, 0),
    (1, 0, 1),
    (1, 0, -1),
    (0, 1, 1),
    (0, 1, -1),
)


def extended(array, sides, width):
    for axis, dim in sides:
        count, length = (lax.axis_size(axis), array.shape[dim])
        up = [(i, (i + 1) % count) for i in range(count - 1)]
        down = [(j, i) for i, j in up]
        last = lax.slice_in_dim(array, length - width, length, axis=dim)
        initial = lax.slice_in_dim(array, 0, width, axis=dim)
        before = lax.ppermute(last, axis, up)
        after = lax.ppermute(initial, axis, down)
        array = jnp.concatenate([before, array, after], axis=dim)
    return array


def crop(array, trim):
    if trim == 0:
        return array
    return array[..., trim:-trim, trim:-trim, trim:-trim]


def shifted(padded, offset):
    sizes = [padded.shape[-3 + axis] - 2 for axis in range(3)]
    starts = [1 + offset[axis] for axis in range(3)]
    return padded[
        ...,
        starts[0] : starts[0] + sizes[0],
        starts[1] : starts[1] + sizes[1],
        starts[2] : starts[2] + sizes[2],
    ]


def neighbour_terms(field_pad, tissue_pad, flux_pad):
    centre = crop(field_pad, 1)
    tissue_mid = crop(tissue_pad, 1)
    flux_mid = crop(flux_pad, 1)
    total = jnp.zeros_like(centre)
    for direction, base in enumerate(PAIR_OFFSETS):
        for sign in (1, -1):
            offset = tuple((sign * part for part in base))
            coupling = 0.5 * (
                flux_mid[direction] * shifted(tissue_pad, offset)
                + shifted(flux_pad[direction], offset) * tissue_mid
            )
            total = total + coupling * (shifted(field_pad, offset) - centre)
    return total


def region_terms(adjoint_pad, field_pad, tissue_pad, fibre_mid):
    adjoint_mid = crop(adjoint_pad, 1)
    centre = crop(field_pad, 1)
    total = jnp.zeros_like(centre)
    for direction, base in enumerate(PAIR_OFFSETS):
        for sign in (1, -1):
            offset = tuple((sign * part for part in base))
            weight = shifted(tissue_pad, offset) * fibre_mid[direction]
            total = total + weight * (shifted(adjoint_pad, offset) - adjoint_mid) * (
                shifted(field_pad, offset) - centre
            )
    return -0.5 * crop(tissue_pad, 1) * total


def ionic(volts, gate_now):
    switch = jax.nn.sigmoid((volts - gate_level) / gate_width)
    drive_v = gate_now * volts * volts * (1.0 - volts) / tau_inward - volts / tau_outward
    drive_h = (1.0 - switch) * (1.0 - gate_now) / tau_opening - switch * gate_now / tau_closing
    return (drive_v, drive_h)


def ionic_partials(volts, gate_now):
    switch = jax.nn.sigmoid((volts - gate_level) / gate_width)
    slope = switch * (1.0 - switch) / gate_width
    deriv_vv = gate_now * (2.0 * volts - 3.0 * volts * volts) / tau_inward - 1.0 / tau_outward
    deriv_vh = volts * volts * (1.0 - volts) / tau_inward
    deriv_hv = slope * (-(1.0 - gate_now) / tau_opening - gate_now / tau_closing)
    deriv_hh = -(1.0 - switch) / tau_opening - switch / tau_closing
    return (deriv_vv, deriv_vh, deriv_hv, deriv_hh)


def forward_step(volts_pad, gate_now, tissue_mid, tissue_pad, flux_pad):
    volts = crop(volts_pad, 1)
    drive_v, drive_h = ionic(volts, gate_now)
    spread = neighbour_terms(volts_pad, tissue_pad, flux_pad)
    return (
        volts + tissue_mid * (spread + step_size * drive_v),
        gate_now + tissue_mid * step_size * drive_h,
    )


def local_coefficients(tissue_mask, fibre_sector, region_label, fibre_table, conductance):
    tissue_local = tissue_mask.astype(jnp.float32)
    local_factor = jnp.zeros(tissue_local.shape, jnp.float32)
    for label in range(conductance.shape[0]):
        local_factor = local_factor + jnp.where(region_label == label, conductance[label], 0.0)
    fibre_local = jnp.zeros((9,) + tissue_local.shape, jnp.float32)
    for label in range(fibre_table.shape[0]):
        fibre_local = fibre_local + jnp.where(
            (fibre_sector == label)[None], fibre_table[label][:, None, None, None], 0.0
        )
    flux_local = (tissue_local * local_factor)[None] * fibre_local
    return (tissue_local, fibre_local, flux_local)


def local(
    potential,
    gating,
    adjoint_v,
    adjoint_h,
    recorded,
    tissue_mask,
    fibre_sector,
    region_label,
    fibre_table,
    conductance,
):
    span = 1
    tissue_local, fibre_mid, flux_local = local_coefficients(
        tissue_mask, fibre_sector, region_label, fibre_table, conductance
    )
    flux_all = extended(flux_local, (("gx", 1), ("gy", 2), ("gz", 3)), span)
    tissue_all = jnp.where(flux_all[0] > 0.0, 1.0, 0.0).astype(jnp.float32)
    tissue_pad = crop(tissue_all, span - 1)
    flux_pad = crop(flux_all, span - 1)
    saved_pads = []
    saved_gates = []
    volts = potential
    gate_now = gating
    for step in range(WINDOW_STEPS):
        volts_pad = extended(volts, (("gx", 0), ("gy", 1), ("gz", 2)), 1)
        saved_pads.append(volts_pad)
        saved_gates.append(gate_now)
        volts, gate_now = forward_step(volts_pad, gate_now, tissue_local, tissue_pad, flux_pad)
    back_v = adjoint_v + tissue_local * (volts - recorded)
    back_h = adjoint_h
    region_count = conductance.shape[0]
    selector = (
        region_label[None] == jnp.arange(region_count, dtype=jnp.int32)[:, None, None, None]
    ).astype(jnp.float32)
    total = jnp.zeros((region_count,), jnp.float32)
    for step in reversed(range(WINDOW_STEPS)):
        masked = tissue_local * back_v
        masked_pad = extended(masked, (("gx", 0), ("gy", 1), ("gz", 2)), 1)
        volts_pad = saved_pads[step]
        terms = region_terms(masked_pad, volts_pad, tissue_pad, fibre_mid)
        partial_sums = jnp.einsum(
            "rxyz,xyz->r", selector, terms, precision=jax.lax.Precision.HIGHEST
        )
        total = total + lax.psum(partial_sums, ("gx", "gy", "gz"))
        deriv_vv, deriv_vh, deriv_hv, deriv_hh = ionic_partials(
            crop(volts_pad, 1), saved_gates[step]
        )
        spread = neighbour_terms(masked_pad, tissue_pad, flux_pad)
        next_v = (
            back_v + spread + step_size * tissue_local * (deriv_vv * back_v + deriv_hv * back_h)
        )
        next_h = back_h + step_size * tissue_local * (deriv_vh * back_v + deriv_hh * back_h)
        back_v, back_h = (next_v, next_h)
    cells = (
        potential.shape[0]
        * potential.shape[1]
        * potential.shape[2]
        * lax.axis_size("gx")
        * lax.axis_size("gy")
        * lax.axis_size("gz")
    )
    scale = gradient_gain / math.sqrt(cells / region_count)
    return (back_v, back_h, total * scale)


def solution(mesh):
    in_specs = (
        P(("twin", "gx"), "gy", "gz"),
        P(("twin", "gx"), "gy", "gz"),
        P(("twin", "gx"), "gy", "gz"),
        P(("twin", "gx"), "gy", "gz"),
        P(("twin", "gx"), "gy", "gz"),
        P(("twin", "gx"), "gy", "gz"),
        P(("twin", "gx"), "gy", "gz"),
        P(("twin", "gx"), "gy", "gz"),
        P("twin", None),
        P("twin"),
    )
    out_specs = (P(("twin", "gx"), "gy", "gz"), P(("twin", "gx"), "gy", "gz"), P("twin"))
    return jax.shard_map(local, mesh=mesh, in_specs=in_specs, out_specs=out_specs, check_vma=False)
```

profile of v0, /device:TPU:0, one launch (start us, length us, event | category | flops | bytes accessed | tf_op | source)
XLA Modules:
  0.0 217.4 jit_solution(543356595917093015)
XLA Ops:
  1.4 4.9 %collective-permute-start.7 = (f32[1,16,128]{2,1,0:T(8,128)S(1)}, f32[1,16,128]{2,1,0:T(8,128)S(1)}, u32[]{:S(2)}, u32[]{:S(2)}) collective-permute-start(f32[1,16,128]{2,1,0:T(8,128)S(1)} %get-tuple-element.115), channel_id=1, source_target_pairs={{0,4},{4,8},{8,12},{1,5},{5,9},{9,13},{2,6},{6,10},{10,14},{3,7},{... | collective-permute-start | bytes 24584 | tf_op jit(solution)/shard_map/ppermute | solution.py:39
  8.7 2.0 fusion.198
  11.6 11.1 %add_multiply_fusion.3 = f32[8,16,128]{2,1,0:T(8,128)S(1)} fusion(s32[8,16,128]{2,1,0:T(8,128)} %param.15, s32[8,16,128]{2,1,0:T(8,128)} %param.17, f32[]{:T(128)} %bitcast.15, f32[]{:T(128)} %bitcast.14, f32[]{:T(128)} %bitcast.13, f32[]{:T(128)} %bitcast.12, f32[]{:T(128)} %bitcast.11, f32[]{:T(128)} %bitcast.10, f32[]{:T(128)} %bitcast.9, f32[]{:T(128)} %bitcast.8, ...), kind=kLoop, calls=%fused_computation.360 | loop fusion | flops 802816 | bytes 196672 | tf_op jit(solution)/shard_map/mul | solution.py:129
  23.8 1.5 collective-permute-start.9
  25.3 1.3 collective-permute-start.8
  26.6 4.4 %collective-permute-start = (f32[9,1,16,128]{3,2,1,0:T(8,128)S(1)}, f32[9,1,16,128]{3,2,1,0:T(8,128)S(1)}, u32[]{:S(2)}, u32[]{:S(2)}) collective-permute-start(f32[9,1,16,128]{3,2,1,0:T(8,128)S(1)} %get-tuple-element.45), channel_id=1, source_target_pairs={{0,4},{4,8},{8,12},{1,5},{5,9},{9,13},{2,6},{6,10},{10,14},{3,7},{... | collective-permute-start | bytes 221192 | tf_op jit(solution)/shard_map/ppermute | solution.py:39
  33.5 4.4 %collective-permute-done.1 = f32[9,1,16,128]{3,2,1,0:T(8,128)S(1)} collective-permute-done((f32[9,1,16,128]{3,2,1,0:T(8,128)S(1)}, f32[9,1,16,128]{3,2,1,0:T(8,128)S(1)}, u32[]{:S(2)}, u32[]{:S(2)}) %collective-permute-start.1) | collective-permute-done | bytes 73760 | tf_op jit(solution)/shard_map/ppermute | solution.py:40
  37.9 1.9 collective-permute-start.2
  41.2 3.4 %collective-permute-start.11 = (f32[10,18,1]{2,1,0:T(8,128)S(1)}, f32[10,18,1]{2,1,0:T(8,128)S(1)}, u32[]{:S(2)}, u32[]{:S(2)}) collective-permute-start(f32[10,18,1]{2,1,0:T(8,128)S(1)} %get-tuple-element.57), channel_id=1, source_target_pairs={{0,1},{2,3},{4,5},{6,7},{8,9},{10,11},{12,13},{14,15},{16,17},{18,... | collective-permute-start | bytes 2168 | tf_op jit(solution)/shard_map/ppermute | solution.py:39
  46.2 1.4 fusion.183
  47.5 2.5 %copy.166 = f32[9,10,18,1]{2,3,1,0:T(1,128)} copy(f32[9,10,18,1]{3,2,1,0:T(8,128)} %get-tuple-element.41) | data formatting | bytes 12960
  51.9 5.8 %collective-permute-start.4 = (f32[9,10,18,1]{2,3,1,0:T(1,128)}, f32[9,10,18,1]{2,3,1,0:T(1,128)}, u32[]{:S(2)}, u32[]{:S(2)}) collective-permute-start(f32[9,10,18,1]{2,3,1,0:T(1,128)} %copy.166), channel_id=1, source_target_pairs={{0,1},{2,3},{4,5},{6,7},{8,9},{10,11},{12,13},{14,15},{16,17},{18,... | collective-permute-start | bytes 19448 | tf_op jit(solution)/shard_map/ppermute | solution.py:39
  59.1 1.4 copy.157
  60.6 2.4 %copy.158 = f32[9,10,18,1]{3,2,1,0:T(8,128)} copy(f32[9,10,18,1]{2,3,1,0:T(1,128)} %collective-permute-done.5) | data formatting | bytes 12960 | tf_op jit(solution)/shard_map/ppermute | solution.py:40
  63.0 2.6 %pad_maximum_fusion = f32[9,10,18,130]{3,2,1,0:T(8,128)S(1)} fusion(f32[9,10,18,1]{3,2,1,0:T(8,128)} %copy.158, f32[9,10,1,128]{3,2,1,0:T(1,128)S(1)} %collective-permute-done.3, f32[9,1,16,128]{3,2,1,0:T(8,128)S(1)} %collective-permute-done.1, f32[9,8,16,128]{3,2,1,0:T(8,128)S(1)} %get-tuple-element.30, f32[9,1,16,128]{3,2,1,0:T(8,128)S(1)} %collective-permute-done, ...), kind=kLoop, calls=%fused_computation | loop fusion | flops 1263600 | bytes 1684800 | tf_op jit(solution)/shard_map/concatenate | solution.py:41
  67.4 3.5 %collective-permute-start.13 = (f32[1,16,128]{2,1,0:T(8,128)S(1)}, f32[1,16,128]{2,1,0:T(8,128)S(1)}, u32[]{:S(2)}, u32[]{:S(2)}) collective-permute-start(f32[1,16,128]{2,1,0:T(8,128)S(1)} %get-tuple-element.101), channel_id=1, source_target_pairs={{0,4},{4,8},{8,12},{1,5},{5,9},{9,13},{2,6},{6,10},{10,14},{3,7},{... | collective-permute-start | bytes 24584 | tf_op jit(solution)/shard_map/ppermute | solution.py:39
  72.3 4.2 %collective-permute-done.12 = f32[1,16,128]{2,1,0:T(8,128)S(1)} collective-permute-done((f32[1,16,128]{2,1,0:T(8,128)S(1)}, f32[1,16,128]{2,1,0:T(8,128)S(1)}, u32[]{:S(2)}, u32[]{:S(2)}) %collective-permute-start.12) | collective-permute-done | bytes 8224 | tf_op jit(solution)/shard_map/ppermute | solution.py:40
  79.1 1.8 collective-permute-done.14
  81.0 4.3 %collective-permute-start.17 = (f32[10,18,1]{2,1,0:T(8,128)S(1)}, f32[10,18,1]{2,1,0:T(8,128)S(1)}, u32[]{:S(2)}, u32[]{:S(2)}) collective-permute-start(f32[10,18,1]{2,1,0:T(8,128)S(1)} %get-tuple-element.55), channel_id=1, source_target_pairs={{0,1},{2,3},{4,5},{6,7},{8,9},{10,11},{12,13},{14,15},{16,17},{18,... | collective-permute-start | bytes 2168 | tf_op jit(solution)/shard_map/ppermute | solution.py:39
  86.6 1.6 collective-permute-done.17
  88.2 4.1 %collective-permute-done.16 = f32[10,18,1]{2,1,0:T(8,128)S(1)} collective-permute-done((f32[10,18,1]{2,1,0:T(8,128)S(1)}, f32[10,18,1]{2,1,0:T(8,128)S(1)}, u32[]{:S(2)}, u32[]{:S(2)}) %collective-permute-start.16) | collective-permute-done | bytes 752 | tf_op jit(solution)/shard_map/ppermute | solution.py:40
  92.8 3.6 %collective-permute-start.19 = (f32[1,16,128]{2,1,0:T(8,128)S(1)}, f32[1,16,128]{2,1,0:T(8,128)S(1)}, u32[]{:S(2)}, u32[]{:S(2)}) collective-permute-start(f32[1,16,128]{2,1,0:T(8,128)S(1)} %get-tuple-element.99), channel_id=1, source_target_pairs={{0,4},{4,8},{8,12},{1,5},{5,9},{9,13},{2,6},{6,10},{10,14},{3,7},{... | collective-permute-start | bytes 24584 | tf_op jit(solution)/shard_map/ppermute | solution.py:39
  97.8 4.2 %collective-permute-done.18 = f32[1,16,128]{2,1,0:T(8,128)S(1)} collective-permute-done((f32[1,16,128]{2,1,0:T(8,128)S(1)}, f32[1,16,128]{2,1,0:T(8,128)S(1)}, u32[]{:S(2)}, u32[]{:S(2)}) %collective-permute-start.18) | collective-permute-done | bytes 8224 | tf_op jit(solution)/shard_map/ppermute | solution.py:40
  104.6 1.8 collective-permute-done.20
  106.5 1.5 collective-permute-start.23
  109.3 1.7 collective-permute-done.23
  111.0 4.1 %collective-permute-done.22 = f32[10,18,1]{2,1,0:T(8,128)S(1)} collective-permute-done((f32[10,18,1]{2,1,0:T(8,128)S(1)}, f32[10,18,1]{2,1,0:T(8,128)S(1)}, u32[]{:S(2)}, u32[]{:S(2)}) %collective-permute-start.22) | collective-permute-done | bytes 752 | tf_op jit(solution)/shard_map/ppermute | solution.py:40
  115.9 1.9 collective-permute-start.25
  119.2 4.2 %collective-permute-done.24 = f32[1,16,128]{2,1,0:T(8,128)S(1)} collective-permute-done((f32[1,16,128]{2,1,0:T(8,128)S(1)}, f32[1,16,128]{2,1,0:T(8,128)S(1)}, u32[]{:S(2)}, u32[]{:S(2)}) %collective-permute-start.24) | collective-permute-done | bytes 8224 | tf_op jit(solution)/shard_map/ppermute | solution.py:40
  124.7 1.4 collective-permute-start.26
  126.3 1.6 collective-permute-done.26
  128.0 1.5 collective-permute-start.29
  130.8 1.7 collective-permute-done.29
  132.5 4.1 %collective-permute-done.28 = f32[10,18,1]{2,1,0:T(8,128)S(1)} collective-permute-done((f32[10,18,1]{2,1,0:T(8,128)S(1)}, f32[10,18,1]{2,1,0:T(8,128)S(1)}, u32[]{:S(2)}, u32[]{:S(2)}) %collective-permute-start.28) | collective-permute-done | bytes 752 | tf_op jit(solution)/shard_map/ppermute | solution.py:40
  137.4 1.9 collective-permute-start.31
  141.4 3.5 %collective-permute-done.30 = f32[1,16,128]{2,1,0:T(8,128)S(1)} collective-permute-done((f32[1,16,128]{2,1,0:T(8,128)S(1)}, f32[1,16,128]{2,1,0:T(8,128)S(1)}, u32[]{:S(2)}, u32[]{:S(2)}) %collective-permute-start.30) | collective-permute-done | bytes 8224 | tf_op jit(solution)/shard_map/ppermute | solution.py:40
  146.2 1.5 collective-permute-start.32
  149.4 1.5 collective-permute-start.35
  152.2 1.9 collective-permute-done.35
  154.0 4.1 %collective-permute-done.34 = f32[10,18,1]{2,1,0:T(8,128)S(1)} collective-permute-done((f32[10,18,1]{2,1,0:T(8,128)S(1)}, f32[10,18,1]{2,1,0:T(8,128)S(1)}, u32[]{:S(2)}, u32[]{:S(2)}) %collective-permute-start.34) | collective-permute-done | bytes 752 | tf_op jit(solution)/shard_map/ppermute | solution.py:40
  159.3 1.9 collective-permute-start.37
  163.1 3.6 %collective-permute-done.36 = f32[1,16,128]{2,1,0:T(8,128)S(1)} collective-permute-done((f32[1,16,128]{2,1,0:T(8,128)S(1)}, f32[1,16,128]{2,1,0:T(8,128)S(1)}, u32[]{:S(2)}, u32[]{:S(2)}) %collective-permute-start.36) | collective-permute-done | bytes 8224 | tf_op jit(solution)/shard_map/ppermute | solution.py:40
  171.2 1.5 collective-permute-start.41
  174.0 2.0 collective-permute-done.41
  176.0 4.1 %collective-permute-done.40 = f32[10,18,1]{2,1,0:T(8,128)S(1)} collective-permute-done((f32[10,18,1]{2,1,0:T(8,128)S(1)}, f32[10,18,1]{2,1,0:T(8,128)S(1)}, u32[]{:S(2)}, u32[]{:S(2)}) %collective-permute-start.40) | collective-permute-done | bytes 752 | tf_op jit(solution)/shard_map/ppermute | solution.py:40
  182.3 1.7 fusion.20
  183.9 29.5 %psum.25 = f32[16]{0:T(128)S(1)} all-reduce(f32[16]{0:T(128)S(1)} %fusion), channel_id=1, replica_groups=mesh['twin'=2,'gx'=4,'gy'=2,'gz'=2] {'gx','gy','gz'}, use_global_device_ids=true, to_apply=%region_0.1 | all-reduce | flops 16 | bytes 128 | tf_op jit(solution)/shard_map/psum | solution.py:177
  214.0 3.4 %fusion.14 = f32[8,16,128]{2,1,0:T(8,128)} fusion(f32[8,16,128]{2,1,0:T(8,128)} %param.11, f32[8,16,128]{2,1,0:T(8,128)S(1)} %copy-done.30, f32[8,16,128]{2,1,0:T(8,128)} %copy-done.16, f32[8,16,128]{2,1,0:T(8,128)} %copy-done.15, f32[8,16,128]{2,1,0:T(8,128)} %copy-done.14, f32[8,16,128]{2,1,0:T(8,128)} %copy-done.13, f32[8,16,128]{2,1,0:T(8,128)} %copy-done.12, ...), kind=kLoop, calls=%fused_computation.82 | loop fusion | flops 5701632 | bytes 6291456 | tf_op jit(solution)/shard_map/add | solution.py:183
  (218 shorter events, 49.7 us)
Async XLA Ops:
  1.4 22.3 %collective-permute-start.7 = (f32[1,16,128]{2,1,0:T(8,128)S(1)}, f32[1,16,128]{2,1,0:T(8,128)S(1)}, u32[]{:S(2)}, u32[]{:S(2)}) collective-permute-start(f32[1,16,128]{2,1,0:T(8,128)S(1)} %get-tuple-element.115), channel_id=1, source_target_pairs={{0,4},{4,8},{8,12},{1,5},{5,9},{9,13},{2,6},{6,10},{10,14},{3,7},{... | collective-permute-start | bytes 24584 | tf_op jit(solution)/shard_map/ppermute | solution.py:39
  6.4 17.4 %collective-permute-start.6 = (f32[1,16,128]{2,1,0:T(8,128)S(1)}, f32[1,16,128]{2,1,0:T(8,128)S(1)}, u32[]{:S(2)}, u32[]{:S(2)}) collective-permute-start(f32[1,16,128]{2,1,0:T(8,128)S(1)} %get-tuple-element.116), channel_id=1, source_target_pairs={{4,0},{8,4},{12,8},{5,1},{9,5},{13,9},{6,2},{10,6},{14,10},{7,3},{... | collective-permute-start | bytes 24584 | tf_op jit(solution)/shard_map/ppermute | solution.py:40
  23.8 8.5 %collective-permute-start.9 = (f32[10,1,128]{2,1,0:T(1,128)S(1)}, f32[10,1,128]{2,1,0:T(1,128)S(1)}, u32[]{:S(2)}, u32[]{:S(2)}) collective-permute-start(f32[10,1,128]{2,1,0:T(1,128)S(1)} %get-tuple-element.91), channel_id=1, source_target_pairs={{0,2},{1,3},{4,6},{5,7},{8,10},{9,11},{12,14},{13,15},{16,18},{17,... | collective-permute-start | bytes 15368 | tf_op jit(solution)/shard_map/ppermute | solution.py:39
  25.3 7.0 %collective-permute-start.8 = (f32[10,1,128]{2,1,0:T(1,128)S(1)}, f32[10,1,128]{2,1,0:T(1,128)S(1)}, u32[]{:S(2)}, u32[]{:S(2)}) collective-permute-start(f32[10,1,128]{2,1,0:T(1,128)S(1)} %get-tuple-element.92), channel_id=1, source_target_pairs={{2,0},{3,1},{6,4},{7,5},{10,8},{11,9},{14,12},{15,13},{18,16},{19,... | collective-permute-start | bytes 15368 | tf_op jit(solution)/shard_map/ppermute | solution.py:40
  26.6 6.9 %collective-permute-start = (f32[9,1,16,128]{3,2,1,0:T(8,128)S(1)}, f32[9,1,16,128]{3,2,1,0:T(8,128)S(1)}, u32[]{:S(2)}, u32[]{:S(2)}) collective-permute-start(f32[9,1,16,128]{3,2,1,0:T(8,128)S(1)} %get-tuple-element.45), channel_id=1, source_target_pairs={{0,4},{4,8},{8,12},{1,5},{5,9},{9,13},{2,6},{6,10},{10,14},{3,7},{... | collective-permute-start | bytes 221192 | tf_op jit(solution)/shard_map/ppermute | solution.py:39
  31.0 6.9 %collective-permute-start.1 = (f32[9,1,16,128]{3,2,1,0:T(8,128)S(1)}, f32[9,1,16,128]{3,2,1,0:T(8,128)S(1)}, u32[]{:S(2)}, u32[]{:S(2)}) collective-permute-start(f32[9,1,16,128]{3,2,1,0:T(8,128)S(1)} %get-tuple-element.46), channel_id=1, source_target_pairs={{4,0},{8,4},{12,8},{5,1},{9,5},{13,9},{6,2},{10,6},{14,10},{7,3},{... | collective-permute-start | bytes 221192 | tf_op jit(solution)/shard_map/ppermute | solution.py:40
  37.9 8.0 %collective-permute-start.2 = (f32[9,10,1,128]{3,2,1,0:T(1,128)S(1)}, f32[9,10,1,128]{3,2,1,0:T(1,128)S(1)}, u32[]{:S(2)}, u32[]{:S(2)}) collective-permute-start(f32[9,10,1,128]{3,2,1,0:T(1,128)S(1)} %get-tuple-element.43), channel_id=1, source_target_pairs={{0,2},{1,3},{4,6},{5,7},{8,10},{9,11},{12,14},{13,15},{16,18},{17,... | collective-permute-start | bytes 138248 | tf_op jit(solution)/shard_map/ppermute | solution.py:39
  39.8 6.1 %collective-permute-start.3 = (f32[9,10,1,128]{3,2,1,0:T(1,128)S(1)}, f32[9,10,1,128]{3,2,1,0:T(1,128)S(1)}, u32[]{:S(2)}, u32[]{:S(2)}) collective-permute-start(f32[9,10,1,128]{3,2,1,0:T(1,128)S(1)} %get-tuple-element.44), channel_id=1, source_target_pairs={{2,0},{3,1},{6,4},{7,5},{10,8},{11,9},{14,12},{15,13},{18,16},{19,... | collective-permute-start | bytes 138248 | tf_op jit(solution)/shard_map/ppermute | solution.py:40
  41.2 16.5 %collective-permute-start.11 = (f32[10,18,1]{2,1,0:T(8,128)S(1)}, f32[10,18,1]{2,1,0:T(8,128)S(1)}, u32[]{:S(2)}, u32[]{:S(2)}) collective-permute-start(f32[10,18,1]{2,1,0:T(8,128)S(1)} %get-tuple-element.57), channel_id=1, source_target_pairs={{0,1},{2,3},{4,5},{6,7},{8,9},{10,11},{12,13},{14,15},{16,17},{18,... | collective-permute-start | bytes 2168 | tf_op jit(solution)/shard_map/ppermute | solution.py:39
  44.6 13.1 %collective-permute-start.10 = (f32[10,18,1]{2,1,0:T(8,128)S(1)}, f32[10,18,1]{2,1,0:T(8,128)S(1)}, u32[]{:S(2)}, u32[]{:S(2)}) collective-permute-start(f32[10,18,1]{2,1,0:T(8,128)S(1)} %get-tuple-element.58), channel_id=1, source_target_pairs={{1,0},{3,2},{5,4},{7,6},{9,8},{11,10},{13,12},{15,14},{17,16},{19,... | collective-permute-start | bytes 2168 | tf_op jit(solution)/shard_map/ppermute | solution.py:40
  50.6 9.9 %collective-permute-start.5 = (f32[9,10,18,1]{2,3,1,0:T(1,128)S(1)}, f32[9,10,18,1]{2,3,1,0:T(1,128)}, u32[]{:S(2)}, u32[]{:S(2)}) collective-permute-start(f32[9,10,18,1]{2,3,1,0:T(1,128)S(1)} %copy.167), channel_id=1, source_target_pairs={{1,0},{3,2},{5,4},{7,6},{9,8},{11,10},{13,12},{15,14},{17,16},{19,... | collective-permute-start | bytes 19448 | tf_op jit(solution)/shard_map/ppermute | solution.py:40
  51.9 7.2 %collective-permute-start.4 = (f32[9,10,18,1]{2,3,1,0:T(1,128)}, f32[9,10,18,1]{2,3,1,0:T(1,128)}, u32[]{:S(2)}, u32[]{:S(2)}) collective-permute-start(f32[9,10,18,1]{2,3,1,0:T(1,128)} %copy.166), channel_id=1, source_target_pairs={{0,1},{2,3},{4,5},{6,7},{8,9},{10,11},{12,13},{14,15},{16,17},{18,... | collective-permute-start | bytes 19448 | tf_op jit(solution)/shard_map/ppermute | solution.py:39
  67.3 114.7 %copy-start.2 = (f32[8,16,128]{2,1,0:T(8,128)}, f32[8,16,128]{2,1,0:T(8,128)S(1)}, u32[]{:S(2)}) copy-start(f32[8,16,128]{2,1,0:T(8,128)S(1)} %get-tuple-element.15) | copy-start | bytes 196612
  67.3 114.7 %copy-start.3 = (f32[8,16,128]{2,1,0:T(8,128)}, f32[8,16,128]{2,1,0:T(8,128)S(1)}, u32[]{:S(2)}) copy-start(f32[8,16,128]{2,1,0:T(8,128)S(1)} %get-tuple-element.16) | copy-start | bytes 196612
  67.3 114.7 %copy-start.4 = (f32[8,16,128]{2,1,0:T(8,128)}, f32[8,16,128]{2,1,0:T(8,128)S(1)}, u32[]{:S(2)}) copy-start(f32[8,16,128]{2,1,0:T(8,128)S(1)} %get-tuple-element.17) | copy-start | bytes 196612
  67.3 114.7 %copy-start.5 = (f32[8,16,128]{2,1,0:T(8,128)}, f32[8,16,128]{2,1,0:T(8,128)S(1)}, u32[]{:S(2)}) copy-start(f32[8,16,128]{2,1,0:T(8,128)S(1)} %get-tuple-element.18) | copy-start | bytes 196612
  67.3 114.7 %copy-start.6 = (f32[8,16,128]{2,1,0:T(8,128)}, f32[8,16,128]{2,1,0:T(8,128)S(1)}, u32[]{:S(2)}) copy-start(f32[8,16,128]{2,1,0:T(8,128)S(1)} %get-tuple-element.19) | copy-start | bytes 196612
  67.3 114.7 %copy-start.7 = (f32[8,16,128]{2,1,0:T(8,128)}, f32[8,16,128]{2,1,0:T(8,128)S(1)}, u32[]{:S(2)}) copy-start(f32[8,16,128]{2,1,0:T(8,128)S(1)} %get-tuple-element.20) | copy-start | bytes 196612
  67.4 4.8 %collective-permute-start.13 = (f32[1,16,128]{2,1,0:T(8,128)S(1)}, f32[1,16,128]{2,1,0:T(8,128)S(1)}, u32[]{:S(2)}, u32[]{:S(2)}) collective-permute-start(f32[1,16,128]{2,1,0:T(8,128)S(1)} %get-tuple-element.101), channel_id=1, source_target_pairs={{0,4},{4,8},{8,12},{1,5},{5,9},{9,13},{2,6},{6,10},{10,14},{3,7},{... | collective-permute-start | bytes 24584 | tf_op jit(solution)/shard_map/ppermute | solution.py:39
  70.9 5.5 %collective-permute-start.12 = (f32[1,16,128]{2,1,0:T(8,128)S(1)}, f32[1,16,128]{2,1,0:T(8,128)S(1)}, u32[]{:S(2)}, u32[]{:S(2)}) collective-permute-start(f32[1,16,128]{2,1,0:T(8,128)S(1)} %get-tuple-element.102), channel_id=1, source_target_pairs={{4,0},{8,4},{12,8},{5,1},{9,5},{13,9},{6,2},{10,6},{14,10},{7,3},{... | collective-permute-start | bytes 24584 | tf_op jit(solution)/shard_map/ppermute | solution.py:40
  76.5 2.6 %collective-permute-start.15 = (f32[10,1,128]{2,1,0:T(1,128)S(1)}, f32[10,1,128]{2,1,0:T(1,128)S(1)}, u32[]{:S(2)}, u32[]{:S(2)}) collective-permute-start(f32[10,1,128]{2,1,0:T(1,128)S(1)} %get-tuple-element.89), channel_id=1, source_target_pairs={{0,2},{1,3},{4,6},{5,7},{8,10},{9,11},{12,14},{13,15},{16,18},{17,... | collective-permute-start | bytes 15368 | tf_op jit(solution)/shard_map/ppermute | solution.py:39
  77.8 3.1 %collective-permute-start.14 = (f32[10,1,128]{2,1,0:T(1,128)S(1)}, f32[10,1,128]{2,1,0:T(1,128)S(1)}, u32[]{:S(2)}, u32[]{:S(2)}) collective-permute-start(f32[10,1,128]{2,1,0:T(1,128)S(1)} %get-tuple-element.90), channel_id=1, source_target_pairs={{2,0},{3,1},{6,4},{7,5},{10,8},{11,9},{14,12},{15,13},{18,16},{19,... | collective-permute-start | bytes 15368 | tf_op jit(solution)/shard_map/ppermute | solution.py:40
  81.0 7.2 %collective-permute-start.17 = (f32[10,18,1]{2,1,0:T(8,128)S(1)}, f32[10,18,1]{2,1,0:T(8,128)S(1)}, u32[]{:S(2)}, u32[]{:S(2)}) collective-permute-start(f32[10,18,1]{2,1,0:T(8,128)S(1)} %get-tuple-element.55), channel_id=1, source_target_pairs={{0,1},{2,3},{4,5},{6,7},{8,9},{10,11},{12,13},{14,15},{16,17},{18,... | collective-permute-start | bytes 2168 | tf_op jit(solution)/shard_map/ppermute | solution.py:39
  85.3 7.0 %collective-permute-start.16 = (f32[10,18,1]{2,1,0:T(8,128)S(1)}, f32[10,18,1]{2,1,0:T(8,128)S(1)}, u32[]{:S(2)}, u32[]{:S(2)}) collective-permute-start(f32[10,18,1]{2,1,0:T(8,128)S(1)} %get-tuple-element.56), channel_id=1, source_target_pairs={{1,0},{3,2},{5,4},{7,6},{9,8},{11,10},{13,12},{15,14},{17,16},{19,... | collective-permute-start | bytes 2168 | tf_op jit(solution)/shard_map/ppermute | solution.py:40
  92.8 5.0 %collective-permute-start.19 = (f32[1,16,128]{2,1,0:T(8,128)S(1)}, f32[1,16,128]{2,1,0:T(8,128)S(1)}, u32[]{:S(2)}, u32[]{:S(2)}) collective-permute-start(f32[1,16,128]{2,1,0:T(8,128)S(1)} %get-tuple-element.99), channel_id=1, source_target_pairs={{0,4},{4,8},{8,12},{1,5},{5,9},{9,13},{2,6},{6,10},{10,14},{3,7},{... | collective-permute-start | bytes 24584 | tf_op jit(solution)/shard_map/ppermute | solution.py:39
  96.5 5.5 %collective-permute-start.18 = (f32[1,16,128]{2,1,0:T(8,128)S(1)}, f32[1,16,128]{2,1,0:T(8,128)S(1)}, u32[]{:S(2)}, u32[]{:S(2)}) collective-permute-start(f32[1,16,128]{2,1,0:T(8,128)S(1)} %get-tuple-element.100), channel_id=1, source_target_pairs={{4,0},{8,4},{12,8},{5,1},{9,5},{13,9},{6,2},{10,6},{14,10},{7,3},{... | collective-permute-start | bytes 24584 | tf_op jit(solution)/shard_map/ppermute | solution.py:40
  102.0 2.6 %collective-permute-start.21 = (f32[10,1,128]{2,1,0:T(1,128)S(1)}, f32[10,1,128]{2,1,0:T(1,128)S(1)}, u32[]{:S(2)}, u32[]{:S(2)}) collective-permute-start(f32[10,1,128]{2,1,0:T(1,128)S(1)} %get-tuple-element.85), channel_id=1, source_target_pairs={{0,2},{1,3},{4,6},{5,7},{8,10},{9,11},{12,14},{13,15},{16,18},{17,... | collective-permute-start | bytes 15368 | tf_op jit(solution)/shard_map/ppermute | solution.py:39
  103.3 3.1 %collective-permute-start.20 = (f32[10,1,128]{2,1,0:T(1,128)S(1)}, f32[10,1,128]{2,1,0:T(1,128)S(1)}, u32[]{:S(2)}, u32[]{:S(2)}) collective-permute-start(f32[10,1,128]{2,1,0:T(1,128)S(1)} %get-tuple-element.86), channel_id=1, source_target_pairs={{2,0},{3,1},{6,4},{7,5},{10,8},{11,9},{14,12},{15,13},{18,16},{19,... | collective-permute-start | bytes 15368 | tf_op jit(solution)/shard_map/ppermute | solution.py:40
  106.5 4.5 %collective-permute-start.23 = (f32[10,18,1]{2,1,0:T(8,128)S(1)}, f32[10,18,1]{2,1,0:T(8,128)S(1)}, u32[]{:S(2)}, u32[]{:S(2)}) collective-permute-start(f32[10,18,1]{2,1,0:T(8,128)S(1)} %get-tuple-element.53), channel_id=1, source_target_pairs={{0,1},{2,3},{4,5},{6,7},{8,9},{10,11},{12,13},{14,15},{16,17},{18,... | collective-permute-start | bytes 2168 | tf_op jit(solution)/shard_map/ppermute | solution.py:39
  108.0 7.1 %collective-permute-start.22 = (f32[10,18,1]{2,1,0:T(8,128)S(1)}, f32[10,18,1]{2,1,0:T(8,128)S(1)}, u32[]{:S(2)}, u32[]{:S(2)}) collective-permute-start(f32[10,18,1]{2,1,0:T(8,128)S(1)} %get-tuple-element.54), channel_id=1, source_target_pairs={{1,0},{3,2},{5,4},{7,6},{9,8},{11,10},{13,12},{15,14},{17,16},{19,... | collective-permute-start | bytes 2168 | tf_op jit(solution)/shard_map/ppermute | solution.py:40
  115.9 3.3 %collective-permute-start.25 = (f32[1,16,128]{2,1,0:T(8,128)S(1)}, f32[1,16,128]{2,1,0:T(8,128)S(1)}, u32[]{:S(2)}, u32[]{:S(2)}) collective-permute-start(f32[1,16,128]{2,1,0:T(8,128)S(1)} %get-tuple-element.97), channel_id=1, source_target_pairs={{0,4},{4,8},{8,12},{1,5},{5,9},{9,13},{2,6},{6,10},{10,14},{3,7},{... | collective-permute-start | bytes 24584 | tf_op jit(solution)/shard_map/ppermute | solution.py:39
  117.8 5.5 %collective-permute-start.24 = (f32[1,16,128]{2,1,0:T(8,128)S(1)}, f32[1,16,128]{2,1,0:T(8,128)S(1)}, u32[]{:S(2)}, u32[]{:S(2)}) collective-permute-start(f32[1,16,128]{2,1,0:T(8,128)S(1)} %get-tuple-element.98), channel_id=1, source_target_pairs={{4,0},{8,4},{12,8},{5,1},{9,5},{13,9},{6,2},{10,6},{14,10},{7,3},{... | collective-permute-start | bytes 24584 | tf_op jit(solution)/shard_map/ppermute | solution.py:40
  123.4 2.9 %collective-permute-start.27 = (f32[10,1,128]{2,1,0:T(1,128)S(1)}, f32[10,1,128]{2,1,0:T(1,128)S(1)}, u32[]{:S(2)}, u32[]{:S(2)}) collective-permute-start(f32[10,1,128]{2,1,0:T(1,128)S(1)} %get-tuple-element.81), channel_id=1, source_target_pairs={{0,2},{1,3},{4,6},{5,7},{8,10},{9,11},{12,14},{13,15},{16,18},{17,... | collective-permute-start | bytes 15368 | tf_op jit(solution)/shard_map/ppermute | solution.py:39
  124.7 3.2 %collective-permute-start.26 = (f32[10,1,128]{2,1,0:T(1,128)S(1)}, f32[10,1,128]{2,1,0:T(1,128)S(1)}, u32[]{:S(2)}, u32[]{:S(2)}) collective-permute-start(f32[10,1,128]{2,1,0:T(1,128)S(1)} %get-tuple-element.82), channel_id=1, source_target_pairs={{2,0},{3,1},{6,4},{7,5},{10,8},{11,9},{14,12},{15,13},{18,16},{19,... | collective-permute-start | bytes 15368 | tf_op jit(solution)/shard_map/ppermute | solution.py:40
  128.0 4.5 %collective-permute-start.29 = (f32[10,18,1]{2,1,0:T(8,128)S(1)}, f32[10,18,1]{2,1,0:T(8,128)S(1)}, u32[]{:S(2)}, u32[]{:S(2)}) collective-permute-start(f32[10,18,1]{2,1,0:T(8,128)S(1)} %get-tuple-element.51), channel_id=1, source_target_pairs={{0,1},{2,3},{4,5},{6,7},{8,9},{10,11},{12,13},{14,15},{16,17},{18,... | collective-permute-start | bytes 2168 | tf_op jit(solution)/shard_map/ppermute | solution.py:39
  129.4 7.1 %collective-permute-start.28 = (f32[10,18,1]{2,1,0:T(8,128)S(1)}, f32[10,18,1]{2,1,0:T(8,128)S(1)}, u32[]{:S(2)}, u32[]{:S(2)}) collective-permute-start(f32[10,18,1]{2,1,0:T(8,128)S(1)} %get-tuple-element.52), channel_id=1, source_target_pairs={{1,0},{3,2},{5,4},{7,6},{9,8},{11,10},{13,12},{15,14},{17,16},{19,... | collective-permute-start | bytes 2168 | tf_op jit(solution)/shard_map/ppermute | solution.py:40
  137.4 4.0 %collective-permute-start.31 = (f32[1,16,128]{2,1,0:T(8,128)S(1)}, f32[1,16,128]{2,1,0:T(8,128)S(1)}, u32[]{:S(2)}, u32[]{:S(2)}) collective-permute-start(f32[1,16,128]{2,1,0:T(8,128)S(1)} %get-tuple-element.95), channel_id=1, source_target_pairs={{0,4},{4,8},{8,12},{1,5},{5,9},{9,13},{2,6},{6,10},{10,14},{3,7},{... | collective-permute-start | bytes 24584 | tf_op jit(solution)/shard_map/ppermute | solution.py:39
  139.3 5.5 %collective-permute-start.30 = (f32[1,16,128]{2,1,0:T(8,128)S(1)}, f32[1,16,128]{2,1,0:T(8,128)S(1)}, u32[]{:S(2)}, u32[]{:S(2)}) collective-permute-start(f32[1,16,128]{2,1,0:T(8,128)S(1)} %get-tuple-element.96), channel_id=1, source_target_pairs={{4,0},{8,4},{12,8},{5,1},{9,5},{13,9},{6,2},{10,6},{14,10},{7,3},{... | collective-permute-start | bytes 24584 | tf_op jit(solution)/shard_map/ppermute | solution.py:40
  144.9 3.6 %collective-permute-start.33 = (f32[10,1,128]{2,1,0:T(1,128)S(1)}, f32[10,1,128]{2,1,0:T(1,128)S(1)}, u32[]{:S(2)}, u32[]{:S(2)}) collective-permute-start(f32[10,1,128]{2,1,0:T(1,128)S(1)} %get-tuple-element.77), channel_id=1, source_target_pairs={{0,2},{1,3},{4,6},{5,7},{8,10},{9,11},{12,14},{13,15},{16,18},{17,... | collective-permute-start | bytes 15368 | tf_op jit(solution)/shard_map/ppermute | solution.py:39
  146.2 3.1 %collective-permute-start.32 = (f32[10,1,128]{2,1,0:T(1,128)S(1)}, f32[10,1,128]{2,1,0:T(1,128)S(1)}, u32[]{:S(2)}, u32[]{:S(2)}) collective-permute-start(f32[10,1,128]{2,1,0:T(1,128)S(1)} %get-tuple-element.78), channel_id=1, source_target_pairs={{2,0},{3,1},{6,4},{7,5},{10,8},{11,9},{14,12},{15,13},{18,16},{19,... | collective-permute-start | bytes 15368 | tf_op jit(solution)/shard_map/ppermute | solution.py:40
  149.4 4.7 %collective-permute-start.35 = (f32[10,18,1]{2,1,0:T(8,128)S(1)}, f32[10,18,1]{2,1,0:T(8,128)S(1)}, u32[]{:S(2)}, u32[]{:S(2)}) collective-permute-start(f32[10,18,1]{2,1,0:T(8,128)S(1)} %get-tuple-element.49), channel_id=1, source_target_pairs={{0,1},{2,3},{4,5},{6,7},{8,9},{10,11},{12,13},{14,15},{16,17},{18,... | collective-permute-start | bytes 2168 | tf_op jit(solution)/shard_map/ppermute | solution.py:39
  150.8 7.3 %collective-permute-start.34 = (f32[10,18,1]{2,1,0:T(8,128)S(1)}, f32[10,18,1]{2,1,0:T(8,128)S(1)}, u32[]{:S(2)}, u32[]{:S(2)}) collective-permute-start(f32[10,18,1]{2,1,0:T(8,128)S(1)} %get-tuple-element.50), channel_id=1, source_target_pairs={{1,0},{3,2},{5,4},{7,6},{9,8},{11,10},{13,12},{15,14},{17,16},{19,... | collective-permute-start | bytes 2168 | tf_op jit(solution)/shard_map/ppermute | solution.py:40
  159.3 3.8 %collective-permute-start.37 = (f32[1,16,128]{2,1,0:T(8,128)S(1)}, f32[1,16,128]{2,1,0:T(8,128)S(1)}, u32[]{:S(2)}, u32[]{:S(2)}) collective-permute-start(f32[1,16,128]{2,1,0:T(8,128)S(1)} %get-tuple-element.93), channel_id=1, source_target_pairs={{0,4},{4,8},{8,12},{1,5},{5,9},{9,13},{2,6},{6,10},{10,14},{3,7},{... | collective-permute-start | bytes 24584 | tf_op jit(solution)/shard_map/ppermute | solution.py:39
  161.2 5.5 %collective-permute-start.36 = (f32[1,16,128]{2,1,0:T(8,128)S(1)}, f32[1,16,128]{2,1,0:T(8,128)S(1)}, u32[]{:S(2)}, u32[]{:S(2)}) collective-permute-start(f32[1,16,128]{2,1,0:T(8,128)S(1)} %get-tuple-element.94), channel_id=1, source_target_pairs={{4,0},{8,4},{12,8},{5,1},{9,5},{13,9},{6,2},{10,6},{14,10},{7,3},{... | collective-permute-start | bytes 24584 | tf_op jit(solution)/shard_map/ppermute | solution.py:40
  166.7 3.6 %collective-permute-start.39 = (f32[10,1,128]{2,1,0:T(1,128)S(1)}, f32[10,1,128]{2,1,0:T(1,128)S(1)}, u32[]{:S(2)}, u32[]{:S(2)}) collective-permute-start(f32[10,1,128]{2,1,0:T(1,128)S(1)} %get-tuple-element.73), channel_id=1, source_target_pairs={{0,2},{1,3},{4,6},{5,7},{8,10},{9,11},{12,14},{13,15},{16,18},{17,... | collective-permute-start | bytes 15368 | tf_op jit(solution)/shard_map/ppermute | solution.py:39
  168.0 3.1 %collective-permute-start.38 = (f32[10,1,128]{2,1,0:T(1,128)S(1)}, f32[10,1,128]{2,1,0:T(1,128)S(1)}, u32[]{:S(2)}, u32[]{:S(2)}) collective-permute-start(f32[10,1,128]{2,1,0:T(1,128)S(1)} %get-tuple-element.74), channel_id=1, source_target_pairs={{2,0},{3,1},{6,4},{7,5},{10,8},{11,9},{14,12},{15,13},{18,16},{19,... | collective-permute-start | bytes 15368 | tf_op jit(solution)/shard_map/ppermute | solution.py:40
  171.2 4.8 %collective-permute-start.41 = (f32[10,18,1]{2,1,0:T(8,128)S(1)}, f32[10,18,1]{2,1,0:T(8,128)S(1)}, u32[]{:S(2)}, u32[]{:S(2)}) collective-permute-start(f32[10,18,1]{2,1,0:T(8,128)S(1)} %get-tuple-element.47), channel_id=1, source_target_pairs={{0,1},{2,3},{4,5},{6,7},{8,9},{10,11},{12,13},{14,15},{16,17},{18,... | collective-permute-start | bytes 2168 | tf_op jit(solution)/shard_map/ppermute | solution.py:39
  172.7 7.4 %collective-permute-start.40 = (f32[10,18,1]{2,1,0:T(8,128)S(1)}, f32[10,18,1]{2,1,0:T(8,128)S(1)}, u32[]{:S(2)}, u32[]{:S(2)}) collective-permute-start(f32[10,18,1]{2,1,0:T(8,128)S(1)} %get-tuple-element.48), channel_id=1, source_target_pairs={{1,0},{3,2},{5,4},{7,6},{9,8},{11,10},{13,12},{15,14},{17,16},{19,... | collective-permute-start | bytes 2168 | tf_op jit(solution)/shard_map/ppermute | solution.py:40
  (50 other events, 2073.9 us)
where the time goes:
time: 219 us; the launch traced here: 217 us
  starting transfers between devices  78.7 us (36%)
  waiting for transfers between devices  62.6 us (29%)
  blocking collectives  29.5 us (13%)
  other arithmetic  28.1 us (13%)
  local copies, waits for them, and re-layouts  13.7 us (6%)
  matrix products  2.53 us (1%)
  between operations  2.23 us (1%)
    ppermute x21, waiting for transfers between devices, extended(): after = lax.ppermute(initial, axis, down)  51.3 us
    ppermute x21, starting transfers between devices, extended(): before = lax.ppermute(last, axis, up)  51.3 us
    psum x1, blocking collectives, local(): total = total + lax.psum(partial_sums, ('gx', 'gy', 'gz'))  29.5 us
    ppermute x21, starting transfers between devices, extended(): after = lax.ppermute(initial, axis, down)  27.4 us
    mul x2, other arithmetic, local_coefficients(): flux_local = (tissue_local * local_factor)[None] * fibre_local  12.1 us
    ppermute x21, waiting for transfers between devices, extended(): before = lax.ppermute(last, axis, up)  11.3 us
  transfers between devices with their start and end apart: 42, of which 23 were waited for; matrix products, arithmetic and copies ran while one was open for 12% of the time, Pallas kernels for 0%

commit v1 on v0

v1 whole, which is shorter than its diff:
```python
import functools
import math

import jax
import jax.numpy as jnp
from jax import lax
from jax.experimental import pallas as pl
from jax.experimental.pallas import tpu as pltpu
from jax.sharding import PartitionSpec as P

WINDOW_STEPS = 3
HALO = 2 * WINDOW_STEPS
LANES = 128
TILE = 8

step_size = 0.1
tau_inward = 0.3
tau_outward = 6.0
tau_opening = 12.0
tau_closing = 15.0
gate_level = 0.13
gate_width = 0.02
gradient_gain = 30.0
PAIR_OFFSETS = (
    (1, 0, 0),
    (0, 1, 0),
    (0, 0, 1),
    (1, 1, 0),
    (1, -1, 0),
    (1, 0, 1),
    (1, 0, -1),
    (0, 1, 1),
    (0, 1, -1),
)
DIRS = len(PAIR_OFFSETS)
Z_DIRS = tuple(d for d, o in enumerate(PAIR_OFFSETS) if o[2])
Y_DIRS = tuple(d for d, o in enumerate(PAIR_OFFSETS) if o[1])
V, G, S, H, B, A = range(6)
WIDTHS = (HALO, HALO, HALO, HALO - 1, WINDOW_STEPS, WINDOW_STEPS - 1)
STARTS = tuple(sum(WIDTHS[:f]) for f in range(6))
PLANES = sum(WIDTHS)
SLOT = 16


def matchings(count):
    result = []
    for parity in range(0 if count == 1 else 1 if count == 2 else 2):
        partner = [i + 1 if i % 2 == parity else i - 1 for i in range(count)]
        result.append([j if 0 <= j < count else i for i, j in enumerate(partner)])
    return result


def looks_up(axis, parity):
    return lax.rem(lax.axis_index(axis), 2) == parity


def lane_ids(rows):
    return lax.broadcasted_iota(jnp.int32, (rows, LANES), 1)


def aligned(start):
    return start if isinstance(start, int) else pl.multiple_of(start, TILE)


def pack_kernel(nx, cond, pot, gat, adv, adh, rec, mask, sec, reg, *outs):
    sx, (sz,) = outs[:nx], outs[nx : nx + 1]
    sd = outs[nx + 1 : 2 * nx + 1]
    sy, g_out, s_out, b_out = outs[2 * nx + 1 :]
    X, Y, _ = pot.shape
    core = lax.axis_index("gy")
    label = reg[...]
    factor = jnp.zeros(label.shape, jnp.float32)
    for r in range(cond.shape[0]):
        factor = jnp.where(label == r, cond[r], factor)
    m = mask[...].astype(jnp.float32)
    g_out[...] = m * factor
    s_out[...] = sec[...].astype(jnp.float32)
    b_out[...] = adv[...] - m * rec[...]
    fields = (pot, g_out, s_out, gat, b_out, adh)
    for k in range(nx):
        up = looks_up("gx", k)
        for f, w in enumerate(WIDTHS):
            start = jnp.where(up, X - w, 0)
            sx[k][STARTS[f] : STARTS[f] + w] = fields[f][pl.ds(start, w)]
    send_row = pl.multiple_of(TILE * (1 - core), TILE)
    half = Y // 2
    lanes = lane_ids(X * Y)
    packed = pot[...].reshape(X * Y, LANES)
    for f in range(1, 6):
        rolled = pltpu.roll(fields[f][...].reshape(X * Y, LANES), SLOT * f, 1)
        inside = (lanes >= SLOT * f - SLOT // 2) & (lanes < SLOT * f + SLOT // 2)
        packed = jnp.where(inside, rolled, packed)
    sz[...] = packed.reshape(X, Y, LANES)
    for k in range(nx):
        start = jnp.where(looks_up("gx", k), X - HALO, 0)
        sd[k][...] = sz[pl.ds(start, HALO)]
    row = pl.multiple_of(jnp.where(core == 0, Y - TILE, 0), TILE)
    for f in range(6):
        sy[f] = fields[f][:, pl.ds(row, TILE), :]


def z_up(a, h):
    last = lane_ids(a.shape[0]) == LANES - 1
    ra, rh = pltpu.roll(a, LANES - 1, 1), pltpu.roll(h, LANES - 1, 1)
    return jnp.where(last, rh, ra), jnp.where(last, ra, rh)


def z_down(a, h):
    first = lane_ids(a.shape[0]) == 0
    ra, rh = pltpu.roll(a, 1, 1), pltpu.roll(h, 1, 1)
    return jnp.where(first, rh, ra), jnp.where(first, ra, rh)


def window_kernel(nx, nz, sizes, *refs):
    size_x, size_z = sizes
    it = iter(refs)

    def take(n):
        return [next(it) for _ in range(n)]

    tab, reg = take(2)
    own = take(6)
    rx, rz, rd = take(nx), take(nz), take(nx * nz)
    (yo,) = take(1)
    yx, yz, yd = take(nx), take(nz), take(nx * nz)
    out_v, out_h, out_t = take(3)
    U, MU, MK, FL, FZ, K, KZ = take(7)
    EG, ES, EH, EB, EA, SG, AV, AH, Q, RS = take(10)

    X, Y, _ = own[V].shape
    XE, YE = X + 2 * HALO, Y + TILE
    ROW = YE + TILE
    core = lax.axis_index("gy")
    xi, zi = lax.axis_index("gx"), lax.axis_index("gz")
    ro = pl.multiple_of(TILE * core, TILE)
    po = pl.multiple_of(Y * (1 - core), TILE)
    ps = pl.multiple_of((Y - TILE) * 0 + TILE * core * ((Y - TILE) // TILE), TILE)

    def at(x, row=0):
        return aligned(x * ROW + TILE + row)

    def load(ref, index, x, dy=0, rows=None, row=0):
        start = x * ROW + TILE + row + dy
        if not dy:
            start = aligned(start)
        return ref[index + (pl.ds(start, rows or YE), slice(None))]

    blank = jnp.zeros((TILE, LANES), jnp.float32)

    @pl.loop(0, XE + 1)
    def _(x):
        row = pl.multiple_of(x * ROW, TILE)
        for part in range(2):
            for kind in range(3):
                for n in range(WINDOW_STEPS):
                    U[n, kind, part, pl.ds(row, TILE), :] = blank
                    MU[n, kind, part, pl.ds(row, TILE), :] = blank
                MK[kind, part, pl.ds(row, TILE), :] = blank
            for d in Y_DIRS:
                K[d, part, pl.ds(row, TILE), :] = blank
            for i, d in enumerate(Z_DIRS):
                if d in Y_DIRS:
                    KZ[i, part, pl.ds(row, TILE), :] = blank

    stores = {G: EG, S: ES, H: EH, B: EB, A: EA}

    def put(f, part, xe, row, value):
        rows = value.shape[0]
        if f == V:
            U[0, 0, part, pl.ds(at(xe, row), rows), :] = value
        elif f == H:
            EH[0, part, xe, pl.ds(row, rows), :] = value
        else:
            stores[f][part, xe, pl.ds(row, rows), :] = value

    def spread(f, packs):
        parts = [pltpu.roll(p, (LANES - SLOT * f) % LANES, 1) if f else p for p in packs]
        if len(parts) == 1:
            value = parts[0]
        else:
            value = jnp.where(lane_ids(parts[0].shape[0]) < LANES // 2, *[
                jnp.where(looks_up("gz", 0), parts[0], parts[1]),
                jnp.where(looks_up("gz", 0), parts[1], parts[0]),
            ])
        return value

    def lanes_ok(rows):
        lanes = lane_ids(rows)
        right = (lanes < HALO) & (zi < size_z - 1)
        left = (lanes >= LANES - HALO) & (zi > 0)
        return right | left

    if nx < 2 or nz < 1:
        for ref in (EG, ES, EB, EA):
            ref[...] = jnp.zeros(ref.shape, jnp.float32)
        EH[0] = jnp.zeros(EH.shape[1:], jnp.float32)
        for part in range(2):
            U[0, 0, part] = jnp.zeros(U.shape[3:], jnp.float32)

    for f, w in enumerate(WIDTHS):
        for i in range(X):
            put(f, 0, HALO + i, ro, own[f][i])
            put(f, 0, HALO + i, po, yo[f, i])
        for k in range(nx):
            up = looks_up("gx", k)
            ok = jnp.where(up, xi < size_x - 1, xi > 0)
            dest = jnp.where(up, HALO + X, HALO - w)
            for i in range(w):
                mine = rx[k][STARTS[f] + i]
                theirs = yx[k][STARTS[f] + i, pl.ds(ps, TILE), :]
                if f == G:
                    mine, theirs = jnp.where(ok, mine, 0.0), jnp.where(ok, theirs, 0.0)
                put(f, 0, dest + i, ro, mine)
                put(f, 0, dest + i, po, theirs)

    if nz:

        def halo_plane(xe, ok, mine, theirs):
            for f in range(6):
                a, b = spread(f, mine), spread(f, theirs)
                if f == G:
                    a = jnp.where(lanes_ok(Y) & ok, a, 0.0)
                    b = jnp.where(lanes_ok(TILE) & ok, b, 0.0)
                put(f, 1, xe, ro, a)
                put(f, 1, xe, po, b)

        @pl.loop(0, X)
        def _(i):
            halo_plane(
                HALO + i, True, [r[i] for r in rz], [r[i, pl.ds(ps, TILE), :] for r in yz]
            )

        @pl.loop(0, HALO)
        def _(i):
            for k in range(nx):
                up = looks_up("gx", k)
                ok = jnp.where(up, xi < size_x - 1, xi > 0)
                dest = jnp.where(up, HALO + X, 0)
                halo_plane(
                    dest + i,
                    ok,
                    [r[i] for r in rd[k * nz : (k + 1) * nz]],
                    [r[i, pl.ds(ps, TILE), :] for r in yd[k * nz : (k + 1) * nz]],
                )

    def put_kinds(ref, index, x, a, h):
        rows = pl.ds(at(x), YE)
        for kind, (p, q) in enumerate(((a, h), z_up(a, h), z_down(a, h))):
            ref[index + (kind, 0, rows, slice(None))] = p
            ref[index + (kind, 1, rows, slice(None))] = q

    @pl.loop(0, XE)
    def _(x):
        rows = pl.ds(at(x), YE)
        v = [load(U, (0, 0, part), x) for part in range(2)]
        for kind, pair in ((1, z_up(*v)), (2, z_down(*v))):
            for part in range(2):
                U[0, kind, part, rows, :] = pair[part]
        g = [EG[part, x] for part in range(2)]
        put_kinds(MK, (), x, *[jnp.where(t > 0.0, 1.0, 0.0) for t in g])
        sector = [
            jnp.where(g[part] > 0.0, ES[part, x], 0.0).astype(jnp.int32) for part in range(2)
        ]
        for d, (_, _, dz) in enumerate(PAIR_OFFSETS):
            line = jnp.broadcast_to(tab[d : d + 1, :], (YE, LANES))
            flux = [
                g[part] * jnp.take_along_axis(line, sector[part], axis=1) for part in range(2)
            ]
            for part in range(2):
                FL[d, part, rows, :] = flux[part]
            if dz:
                pair = (z_up if dz > 0 else z_down)(*flux)
                for part in range(2):
                    FZ[Z_DIRS.index(d), part, rows, :] = pair[part]

    def kind_of(dz):
        return 0 if dz == 0 else 1 if dz > 0 else 2

    @pl.loop(0, XE - 1)
    def _(x):
        rows = pl.ds(at(x), YE)
        for d, (dx, dy, dz) in enumerate(PAIR_OFFSETS):
            pair = []
            for part in range(2):
                both = load(MK, (0, part), x) * load(MK, (kind_of(dz), part), x + dx, dy)
                there = (
                    load(FZ, (Z_DIRS.index(d), part), x + dx, dy)
                    if dz
                    else load(FL, (d, part), x + dx, dy)
                )
                pair.append(jnp.where(both > 0.0, load(FL, (d, part), x) + there, 0.0))
                K[d, part, rows, :] = pair[part]
            if dz:
                back = (z_down if dz > 0 else z_up)(*pair)
                for part in range(2):
                    KZ[Z_DIRS.index(d), part, rows, :] = back[part]

    def spread_of(ref, index, x, part, rows=None, row=0):
        centre = load(ref, index + (0, part), x, 0, rows, row)
        total = None
        for d, (dx, dy, dz) in enumerate(PAIR_OFFSETS):
            up = load(ref, index + (kind_of(dz), part), x + dx, dy, rows, row)
            term = load(K, (d, part), x, 0, rows, row) * (up - centre)
            total = term if total is None else total + term
            down = load(ref, index + (kind_of(-dz), part), x - dx, -dy, rows, row)
            back = (
                load(KZ, (Z_DIRS.index(d), part), x - dx, -dy, rows, row)
                if dz
                else load(K, (d, part), x - dx, -dy, rows, row)
            )
            total = total + back * (down - centre)
        return centre, total

    for n in range(WINDOW_STEPS):
        reach = HALO - 1 - n
        last = n == WINDOW_STEPS - 1

        @pl.loop(HALO - reach, HALO + X + reach)
        def _(x, n=n, last=last):
            fresh = []
            for part in range(2):
                m = load(MK, (0, part), x)
                v, flow = spread_of(U, (n,), x, part)
                h = EH[n, part, x]
                s = jax.nn.sigmoid((v - gate_level) * (1.0 / gate_width))
                SG[n, part, x] = s
                drive = h * v * v * (1.0 - v) * (1.0 / tau_inward) - v * (1.0 / tau_outward)
                v_new = v + m * (flow + step_size * drive)
                if last:
                    a = EB[part, x] + m * v_new
                    AV[part, x] = a
                    fresh.append(m * a)
                else:
                    drive = (1.0 - s) * (1.0 - h) * (1.0 / tau_opening) - s * h * (
                        1.0 / tau_closing
                    )
                    EH[n + 1, part, x] = h + m * (step_size * drive)
                    fresh.append(v_new)
            if last:
                put_kinds(MU, (n,), x, *fresh)
            else:
                put_kinds(U, (n + 1,), x, *fresh)

    def terms():
        row = ro

        @pl.loop(0, X)
        def _(i):
            x = HALO + i
            mu = [load(MU, (n, 0, 0), x, 0, Y, row) for n in range(WINDOW_STEPS)]
            v = [load(U, (n, 0, 0), x, 0, Y, row) for n in range(WINDOW_STEPS)]
            total = jnp.zeros((Y, LANES), jnp.float32)
            for d, (dx, dy, dz) in enumerate(PAIR_OFFSETS):
                edge = None
                for sign in (1, -1):
                    index = (kind_of(sign * dz), 0)
                    where = (x + sign * dx, sign * dy, Y, row)
                    part = None
                    for n in range(WINDOW_STEPS):
                        term = (load(MU, (n,) + index, *where) - mu[n]) * (
                            load(U, (n,) + index, *where) - v[n]
                        )
                        part = term if part is None else part + term
                    part = part * load(MK, index, *where)
                    edge = part if edge is None else edge + part
                total = total + load(FL, (d, 0), x, 0, Y, row) * edge
            Q[i] = total

        RS[...] = jnp.zeros(RS.shape, jnp.float32)
        label = reg[...]
        for r in range(out_t.shape[0] * 0 + RS.shape[0] // TILE):
            found = jnp.where(label == r, Q[...], 0.0)
            RS[r : r + 1, :] = -jnp.sum(jnp.sum(found, axis=0), axis=0, keepdims=True)
        out_t[...] = lax.dot_general(
            jnp.ones((out_t.shape[0], LANES), jnp.float32),
            RS[...],
            (((1,), (1,)), ((), ())),
            precision=lax.Precision.HIGHEST,
            preferred_element_type=jnp.float32,
        )

    for n in reversed(range(WINDOW_STEPS)):
        if n == 0:
            terms()
        first, final = n == WINDOW_STEPS - 1, n == 0

        @pl.loop(HALO - n, HALO + X + n)
        def _(x, n=n, first=first, final=final):
            fresh = []
            for part in range(1 if final else 2):
                rows, row = (Y, ro) if final else (YE, 0)
                here = pl.ds(row, rows)
                m = load(MK, (0, part), x, 0, rows, row)
                v = load(U, (n, 0, part), x, 0, rows, row)
                h = EH[n, part, x, here, :]
                s = SG[n, part, x, here, :]
                a = AV[part, x, here, :]
                e = EA[part, x, here, :] if first else AH[part, x, here, :]
                _, flow = spread_of(MU, (n,), x, part, rows, row)
                slope = s * (1.0 - s) * (1.0 / gate_width)
                f_v = h * (2.0 * v - 3.0 * v * v) * (1.0 / tau_inward) - 1.0 / tau_outward
                f_h = v * v * (1.0 - v) * (1.0 / tau_inward)
                g_v = slope * ((h - 1.0) * (1.0 / tau_opening) - h * (1.0 / tau_closing))
                g_h = (s - 1.0) * (1.0 / tau_opening) - s * (1.0 / tau_closing)
                step = step_size * m
                a_new = a + flow + step * (f_v * a + g_v * e)
                e_new = e + step * (f_h * a + g_h * e)
                if final:
                    out_v[x - HALO] = a_new
                    out_h[x - HALO] = e_new
                else:
                    AV[part, x] = a_new
                    AH[part, x] = e_new
                    fresh.append(m * a_new)
            if not final:
                put_kinds(MU, (n - 1,), x, *fresh)


def vmem(n):
    return [pl.BlockSpec(memory_space=pltpu.VMEM)] * n


def local(pot, gat, adv, adh, rec, mask, sec, reg, table, cond):
    X, Y, Z = pot.shape
    size_x, size_y, size_z = (lax.axis_size(a) for a in ("gx", "gy", "gz"))
    assert size_y == 2 and Z == LANES and X >= HALO and Y % TILE == 0 and Y >= TILE
    assert table.shape[0] <= LANES and cond.shape[0] <= SLOT
    mx, mz = matchings(size_x), matchings(size_z)
    nx, nz = len(mx), len(mz)
    f32 = jnp.float32
    block = jax.ShapeDtypeStruct((X, Y, Z), f32)
    packed = pl.pallas_call(
        functools.partial(pack_kernel, nx),
        out_shape=[jax.ShapeDtypeStruct((PLANES, Y, Z), f32)] * nx
        + [block]
        + [jax.ShapeDtypeStruct((HALO, Y, Z), f32)] * nx
        + [jax.ShapeDtypeStruct((6, X, TILE, Z), f32), block, block, block],
        in_specs=[pl.BlockSpec(memory_space=pltpu.SMEM)] + vmem(8),
        out_specs=vmem(2 * nx + 5),
        name="pack",
    )(cond, pot, gat, adv, adh, rec, mask, sec, reg)
    sx, sz, sd = packed[:nx], packed[nx], packed[nx + 1 : 2 * nx + 1]
    sy, g, s, b = packed[2 * nx + 1 :]

    rx = [lax.ppermute(sx[k], "gx", list(enumerate(mx[k]))) for k in range(nx)]
    rz = [lax.ppermute(sz, "gz", list(enumerate(mz[k]))) for k in range(nz)]
    rd = []
    for kx in range(nx):
        for kz in range(nz):
            pairs = [
                (i * size_z + k, mx[kx][i] * size_z + mz[kz][k])
                for i in range(size_x)
                for k in range(size_z)
            ]
            rd.append(lax.ppermute(sd[kx], ("gx", "gz"), pairs))
    swap = [(0, 1), (1, 0)]
    over = lambda arrays: [lax.ppermute(a, "gy", swap) for a in arrays]
    (yo,) = over([sy])
    yx, yz, yd = over(rx), over(rz), over(rd)

    tab = jnp.pad(0.5 * table.T, ((0, 16 - DIRS), (0, LANES - table.shape[0])))
    devices = size_x * size_y * size_z
    XE, YE = X + 2 * HALO, Y + TILE
    rows = XE * (YE + TILE) + 2 * TILE
    pad = lambda *lead: pltpu.VMEM(lead + (2, rows, LANES), f32)
    ext = lambda *lead: pltpu.VMEM(lead + (2, XE, YE, LANES), f32)
    steps = WINDOW_STEPS
    regions = cond.shape[0]
    operands = [tab, reg, pot, g, s, gat, b, adh, *rx, *rz, *rd, yo, *yx, *yz, *yd]
    lam_v, lam_h, tot = pl.pallas_call(
        functools.partial(window_kernel, nx, nz, (size_x, size_z)),
        out_shape=[block, block, jax.ShapeDtypeStruct((devices, LANES), f32)],
        in_specs=vmem(len(operands)),
        out_specs=vmem(3),
        scratch_shapes=[
            pad(steps, 3), pad(steps, 3), pad(3), pad(DIRS), pad(len(Z_DIRS)),
            pad(DIRS), pad(len(Z_DIRS)),
            ext(), ext(), ext(steps), ext(), ext(), ext(steps), ext(), ext(),
            pltpu.VMEM((X, Y, LANES), f32), pltpu.VMEM((LANES, LANES), f32),
        ],
        compiler_params=pltpu.CompilerParams(vmem_limit_bytes=52 << 20),
        name="window",
    )(*operands)
    every = lax.all_to_all(tot.reshape(devices, 1, LANES), ("gx", "gy", "gz"), 0, 0)
    cells = X * Y * Z * devices
    scale = gradient_gain / math.sqrt(cells / regions)
    total = jnp.sum(every, axis=(0, 1))[:regions] * (scale / cond)
    return lam_v, lam_h, total


def solution(mesh):
    cells = P(("twin", "gx"), "gy", "gz")
    in_specs = (cells,) * 8 + (P("twin", None), P("twin"))
    out_specs = (cells, cells, P("twin"))
    return jax.shard_map(local, mesh=mesh, in_specs=in_specs, out_specs=out_specs, check_vma=False)
```

time: 219 us -> 57.3 us (0.26)
  starting transfers between devices: 78.7 us -> 12.3 us
  waiting for transfers between devices: 62.6 us -> 3.52 us
  other arithmetic: 28.1 us -> 0.56 us
  Pallas kernels: 0 us -> 26.3 us
  blocking collectives: 29.5 us -> 10.2 us
  local copies, waits for them, and re-layouts: 13.7 us -> 3.25 us
  matrix products: 2.53 us -> 0 us
    ppermute x42 -> x11, starting transfers between devices: 78.7 us -> 12.3 us  [the longest x2 5.95 us: local(): rd.append(lax.ppermute(sd[kx], ('gx', 'gz'), pairs))]
    ppermute x42 -> x11, waiting for transfers between devices: 62.6 us -> 3.52 us  [the longest x2 2.29 us: local(): rd.append(lax.ppermute(sd[kx], ('gx', 'gz'), pairs))]
    psum x1 -> x0, blocking collectives: 29.5 us -> none  [local(): total = total + lax.psum(partial_sums, ('gx', 'gy', 'gz'))]
    pallas_call x0 -> x2, Pallas kernels: none -> 26.3 us  [the longest x1 24.1 us: local(): pl.pallas_call(functools.partial(window_kernel, nx, nz, (size_x, size_z))...]
    mul x9 -> x2, other arithmetic: 16.7 us -> 0.52 us  [the longest x1 0.52 us: local(): total = jnp.sum(every, axis=(0, 1))[:regions] * (scale / cond)]
    all_to_all x0 -> x1, blocking collectives: none -> 10.2 us  [local(): lax.all_to_all(tot.reshape(devices, 1, LANES), ('gx', 'gy', 'gz'), 0, 0)]
    add x4 -> x0, other arithmetic: 6.12 us -> none  [the longest x1 3.36 us: local(): back_v + spread]
    slice x16 -> x0, local copies, waits for them, and re-layouts: 4.65 us -> none  [the longest x15 2.69 us: extended(): last = lax.slice_in_dim(array, length - width, length, axis=dim)]
  transfers between devices with their start and end apart: 42 -> 11, of which waited for: 23 -> 4; matrix products, arithmetic and copies ran while one was open for 12% -> 0% of each run, Pallas kernels for 0% -> 0%
where the time goes in v1:
time: 57.3 us; the launch traced here: 56.9 us
  Pallas kernels  26.3 us (46%)
  starting transfers between devices  12.3 us (21%)
  blocking collectives  10.2 us (18%)
  waiting for transfers between devices  3.52 us (6%)
  local copies, waits for them, and re-layouts  3.25 us (6%)
  between operations  0.73 us (1%)
    pallas_call x1, Pallas kernels, local(): pl.pallas_call(functools.partial(window_kernel, nx, nz, (size_x, size_z))...  24.1 us
    all_to_all x1, blocking collectives, local(): lax.all_to_all(tot.reshape(devices, 1, LANES), ('gx', 'gy', 'gz'), 0, 0)  10.2 us
    ppermute x2, starting transfers between devices, local(): rd.append(lax.ppermute(sd[kx], ('gx', 'gz'), pairs))  5.95 us
    ppermute x2, starting transfers between devices, local(): rx = [lax.ppermute(sx[k], 'gx', list(enumerate(mx[k]))) for k in range(nx)]  4.7 us
    unnamed x19, local copies, waits for them, and re-layouts  3.25 us
    ppermute x2, waiting for transfers between devices, local(): rd.append(lax.ppermute(sd[kx], ('gx', 'gz'), pairs))  2.29 us
    pallas_call x1, Pallas kernels, local(): pl.pallas_call(functools.partial(pack_kernel, nx), out_shape=[jax.ShapeDt...  2.19 us
    ppermute x6, waiting for transfers between devices, local(): over = lambda arrays: [lax.ppermute(a, 'gy', swap) for a in arrays]  1.23 us
  transfers between devices with their start and end apart: 11, of which 4 were waited for; matrix products, arithmetic and copies ran while one was open for 0% of the time, Pallas kernels for 0%

profile of v1, /device:TPU:0, one launch (start us, length us, event | category | flops | bytes accessed | tf_op | source)
XLA Modules:
  0.0 56.9 jit_solution(6198140491772589789)
XLA Ops:
  0.6 0.0 copy-start.7
  0.6 0.0 copy-start.1
  0.7 0.0 copy-start.2
  0.7 0.0 copy-start.3
  0.7 2.2 %pack.1 = (f32[28,16,128]{2,1,0:T(8,128)}, f32[28,16,128]{2,1,0:T(8,128)}, f32[8,16,128]{2,1,0:T(8,128)}, f32[6,16,128]{2,1,0:T(8,128)}, f32[6,16,128]{2,1,0:T(8...) custom-call(f32[16]{0:T(128)} %cond.1, ...), custom_call_target="tpu_custom_call" | custom-call | tf_op jit(solution)/shard_map/pack/pallas_call | solution.py:432
  2.9 0.0 copy-start
  2.9 3.1 %collective-permute-start = (f32[28,16,128]{2,1,0:T(8,128)}, f32[28,16,128]{2,1,0:T(8,128)S(1)}, u32[]{:S(2)}, u32[]{:S(2)}) collective-permute-start(f32[28,16,128]{2,1,0:T(8,128)} %get-tuple-element.18), channel_id=1, source_target_pairs={{0,4},{4,0},{8,12},{12,8},{1,5},{5,1},{9,13},{13,9},{2,6},{6,2},{1... | collective-permute-start | bytes 688136 | tf_op jit(solution)/shard_map/ppermute | solution.py:445
  6.0 1.6 %collective-permute-start.1 = (f32[28,16,128]{2,1,0:T(8,128)}, f32[28,16,128]{2,1,0:T(8,128)S(1)}, u32[]{:S(2)}, u32[]{:S(2)}) collective-permute-start(f32[28,16,128]{2,1,0:T(8,128)} %get-tuple-element.19), channel_id=1, source_target_pairs={{0,0},{4,8},{8,4},{12,12},{1,1},{5,9},{9,5},{13,13},{2,2},{6,10},{... | collective-permute-start | bytes 688136 | tf_op jit(solution)/shard_map/ppermute | solution.py:445
  7.6 4.5 %collective-permute-start.3 = (f32[6,16,128]{2,1,0:T(8,128)}, f32[6,16,128]{2,1,0:T(8,128)S(1)}, u32[]{:S(2)}, u32[]{:S(2)}) collective-permute-start(f32[6,16,128]{2,1,0:T(8,128)} %get-tuple-element.21), channel_id=1, source_target_pairs={{0,5},{1,4},{4,1},{5,0},{8,13},{9,12},{12,9},{13,8},{2,7},{3,6},{6... | collective-permute-start | bytes 147464 | tf_op jit(solution)/shard_map/ppermute | solution.py:455
  12.0 0.5 collective-permute-start.2
  12.6 1.5 %collective-permute-start.4 = (f32[6,16,128]{2,1,0:T(8,128)}, f32[6,16,128]{2,1,0:T(8,128)S(1)}, u32[]{:S(2)}, u32[]{:S(2)}) collective-permute-start(f32[6,16,128]{2,1,0:T(8,128)} %get-tuple-element.22), channel_id=1, source_target_pairs={{0,1},{1,0},{4,9},{5,8},{8,5},{9,4},{12,13},{13,12},{2,3},{3,2},{6... | collective-permute-start | bytes 147464 | tf_op jit(solution)/shard_map/ppermute | solution.py:455
  14.1 0.3 collective-permute-done.3.refs_11_
  14.4 0.0 collective-permute-start.9
  14.4 0.0 collective-permute-done.refs_8_
  14.4 0.5 collective-permute-start.6
  14.9 0.0 collective-permute-done.1.refs_9_
  14.9 0.1 collective-permute-start.7
  15.0 0.0 copy-done.7
  15.0 0.1 copy.14
  15.0 2.0 %collective-permute-done.4.refs_12_ = f32[6,16,128]{2,1,0:T(8,128)S(1)} collective-permute-done((f32[6,16,128]{2,1,0:T(8,128)}, f32[6,16,128]{2,1,0:T(8,128)S(1)}, u32[]{:S(2)}, u32[]{:S(2)}) %collective-permute-start.4) | collective-permute-done | bytes 49184 | tf_op jit(solution)/shard_map/ppermute | solution.py:455
  17.0 0.0 collective-permute-start.5
  17.0 0.0 collective-permute-done.2.refs_10_
  17.0 0.5 collective-permute-start.10
  17.6 0.0 collective-permute-done.9.refs_17_
  17.6 0.1 collective-permute-start.8
  17.6 1.1 %collective-permute-done.10.refs_18_ = f32[6,16,128]{2,1,0:T(8,128)S(1)} collective-permute-done((f32[6,16,128]{2,1,0:T(8,128)S(1)}, f32[6,16,128]{2,1,0:T(8,128)S(1)}, u32[]{:S(2)}, u32[]{:S(2)}) %collective-permute-start.10) | collective-permute-done | bytes 49184 | tf_op jit(solution)/shard_map/ppermute | solution.py:457
  18.8 0.1 collective-permute-done.8.refs_16_
  18.9 0.0 collective-permute-done.5.refs_13_
  18.9 0.0 collective-permute-done.6.refs_14_
  18.9 0.0 collective-permute-done.7.refs_15_
  18.9 0.0 copy-done.1
  18.9 0.0 copy-done.2
  18.9 0.0 copy-done.3
  18.9 0.0 copy-done
  18.9 0.0 copy-start.4
  18.9 0.8 %copy-done.4 = f32[8,16,128]{2,1,0:T(8,128)S(1)} copy-done((f32[8,16,128]{2,1,0:T(8,128)S(1)}, f32[8,16,128]{2,1,0:T(8,128)}, u32[]{:S(2)}) %copy-start.4) | copy-done | bytes 65560
  19.8 0.0 copy-start.5
  19.8 0.8 %copy-done.5 = f32[8,16,128]{2,1,0:T(8,128)S(1)} copy-done((f32[8,16,128]{2,1,0:T(8,128)S(1)}, f32[8,16,128]{2,1,0:T(8,128)}, u32[]{:S(2)}) %copy-start.5) | copy-done | bytes 65560
  20.6 0.0 copy-start.6
  20.6 0.8 %copy-done.6 = f32[8,16,128]{2,1,0:T(8,128)S(1)} copy-done((f32[8,16,128]{2,1,0:T(8,128)S(1)}, f32[8,16,128]{2,1,0:T(8,128)}, u32[]{:S(2)}) %copy-start.6) | copy-done | bytes 65560
  21.4 24.1 %window.1 = (f32[8,16,128]{2,1,0:T(8,128)}, f32[8,16,128]{2,1,0:T(8,128)}, f32[16,128]{1,0:T(8,128)S(1)}) custom-call(f32[16,128]{1,0:T(8,128)S(1)} %pad.4.refs_0_, s32[8,16,128]{2,1,0:T(8,128)S(1)} %copy-done, f32[8,16,128]{2,1,0:T(8,128)S(1)} %copy-done.1, f32[8,16,128]{2,1,0:T(8,128)S(1)} %copy-done.4, f32[8,16,128]{2,1,0:T(8,128)S(1)} %copy-done.5, ...), custom_call_target="tpu_custom_call" | custom-call | tf_op jit(solution)/shard_map/window/pallas_call | solution.py:470
  45.5 10.2 %all_to_all.5 = f32[16,1,128]{2,1,0:T(1,128)S(1)} all-to-all(f32[16,1,128]{2,1,0:T(1,128)S(1)} %bitcast.5), channel_id=1, replica_groups=mesh['twin'=2,'gx'=4,'gy'=2,'gz'=2] {'gx','gy','gz'}, dimensions={0} | all-to-all | bytes 16384 | tf_op jit(solution)/shard_map/all_to_all | solution.py:484
  55.7 0.0 copy-start.8
  55.8 0.6 %copy-done.8 = f32[16]{0:T(128)S(1)} copy-done((f32[16]{0:T(128)S(1)}, f32[16]{0:T(128)}, u32[]{:S(2)}) %copy-start.8) | copy-done | bytes 88
  56.4 0.5 divide_multiply_fusion
  (3 shorter events, 0.0 us)
Async XLA Ops:
  0.6 14.3 %copy-start.7 = (f32[12,9]{1,0:T(8,128)S(1)}, f32[12,9]{1,0:T(8,128)}, u32[]{:S(2)}) copy-start(f32[12,9]{1,0:T(8,128)} %param.18) | copy-start | bytes 1300
  0.6 18.2 %copy-start.1 = (f32[8,16,128]{2,1,0:T(8,128)S(1)}, f32[8,16,128]{2,1,0:T(8,128)}, u32[]{:S(2)}) copy-start(f32[8,16,128]{2,1,0:T(8,128)} %refs_2_.1) | copy-start | bytes 196612
  0.7 18.2 %copy-start.2 = (f32[8,16,128]{2,1,0:T(8,128)S(1)}, f32[8,16,128]{2,1,0:T(8,128)}, u32[]{:S(2)}) copy-start(f32[8,16,128]{2,1,0:T(8,128)} %refs_5_.1) | copy-start | bytes 196612
  0.7 18.2 %copy-start.3 = (f32[8,16,128]{2,1,0:T(8,128)S(1)}, f32[8,16,128]{2,1,0:T(8,128)}, u32[]{:S(2)}) copy-start(f32[8,16,128]{2,1,0:T(8,128)} %refs_7_.1) | copy-start | bytes 196612
  2.9 16.0 %copy-start = (s32[8,16,128]{2,1,0:T(8,128)S(1)}, s32[8,16,128]{2,1,0:T(8,128)}, u32[]{:S(2)}) copy-start(s32[8,16,128]{2,1,0:T(8,128)} %refs_1_.1) | copy-start | bytes 196612
  2.9 11.5 %collective-permute-start = (f32[28,16,128]{2,1,0:T(8,128)}, f32[28,16,128]{2,1,0:T(8,128)S(1)}, u32[]{:S(2)}, u32[]{:S(2)}) collective-permute-start(f32[28,16,128]{2,1,0:T(8,128)} %get-tuple-element.18), channel_id=1, source_target_pairs={{0,4},{4,0},{8,12},{12,8},{1,5},{5,1},{9,13},{13,9},{2,6},{6,2},{1... | collective-permute-start | bytes 688136 | tf_op jit(solution)/shard_map/ppermute | solution.py:445
  6.0 8.9 %collective-permute-start.1 = (f32[28,16,128]{2,1,0:T(8,128)}, f32[28,16,128]{2,1,0:T(8,128)S(1)}, u32[]{:S(2)}, u32[]{:S(2)}) collective-permute-start(f32[28,16,128]{2,1,0:T(8,128)} %get-tuple-element.19), channel_id=1, source_target_pairs={{0,0},{4,8},{8,4},{12,12},{1,1},{5,9},{9,5},{13,13},{2,2},{6,10},{... | collective-permute-start | bytes 688136 | tf_op jit(solution)/shard_map/ppermute | solution.py:445
  7.6 6.8 %collective-permute-start.3 = (f32[6,16,128]{2,1,0:T(8,128)}, f32[6,16,128]{2,1,0:T(8,128)S(1)}, u32[]{:S(2)}, u32[]{:S(2)}) collective-permute-start(f32[6,16,128]{2,1,0:T(8,128)} %get-tuple-element.21), channel_id=1, source_target_pairs={{0,5},{1,4},{4,1},{5,0},{8,13},{9,12},{12,9},{13,8},{2,7},{3,6},{6... | collective-permute-start | bytes 147464 | tf_op jit(solution)/shard_map/ppermute | solution.py:455
  12.0 5.0 %collective-permute-start.2 = (f32[8,16,128]{2,1,0:T(8,128)}, f32[8,16,128]{2,1,0:T(8,128)S(1)}, u32[]{:S(2)}, u32[]{:S(2)}) collective-permute-start(f32[8,16,128]{2,1,0:T(8,128)} %get-tuple-element.20), channel_id=1, source_target_pairs={{0,1},{1,0},{2,3},{3,2},{4,5},{5,4},{6,7},{7,6},{8,9},{9,8},{10,11... | collective-permute-start | bytes 196616 | tf_op jit(solution)/shard_map/ppermute | solution.py:446
  12.6 4.5 %collective-permute-start.4 = (f32[6,16,128]{2,1,0:T(8,128)}, f32[6,16,128]{2,1,0:T(8,128)S(1)}, u32[]{:S(2)}, u32[]{:S(2)}) collective-permute-start(f32[6,16,128]{2,1,0:T(8,128)} %get-tuple-element.22), channel_id=1, source_target_pairs={{0,1},{1,0},{4,9},{5,8},{8,5},{9,4},{12,13},{13,12},{2,3},{3,2},{6... | collective-permute-start | bytes 147464 | tf_op jit(solution)/shard_map/ppermute | solution.py:455
  14.4 3.2 %collective-permute-start.9 = (f32[6,16,128]{2,1,0:T(8,128)S(1)}, f32[6,16,128]{2,1,0:T(8,128)S(1)}, u32[]{:S(2)}, u32[]{:S(2)}) collective-permute-start(f32[6,16,128]{2,1,0:T(8,128)S(1)} %collective-permute-done.3.refs_11_), channel_id=1, source_target_pairs={{0,2},{2,0},{1,3},{3,1},{4,6},{6,4},{5,7},{7,5},{8,10},{10,8},{9,1... | collective-permute-start | bytes 147464 | tf_op jit(solution)/shard_map/ppermute | solution.py:457
  14.4 4.5 %collective-permute-start.6 = (f32[28,16,128]{2,1,0:T(8,128)S(1)}, f32[28,16,128]{2,1,0:T(8,128)S(1)}, u32[]{:S(2)}, u32[]{:S(2)}) collective-permute-start(f32[28,16,128]{2,1,0:T(8,128)S(1)} %collective-permute-done.refs_8_), channel_id=1, source_target_pairs={{0,2},{2,0},{1,3},{3,1},{4,6},{6,4},{5,7},{7,5},{8,10},{10,8},{9,1... | collective-permute-start | bytes 688136 | tf_op jit(solution)/shard_map/ppermute | solution.py:457
  14.9 4.0 %collective-permute-start.7 = (f32[28,16,128]{2,1,0:T(8,128)S(1)}, f32[28,16,128]{2,1,0:T(8,128)S(1)}, u32[]{:S(2)}, u32[]{:S(2)}) collective-permute-start(f32[28,16,128]{2,1,0:T(8,128)S(1)} %collective-permute-done.1.refs_9_), channel_id=1, source_target_pairs={{0,2},{2,0},{1,3},{3,1},{4,6},{6,4},{5,7},{7,5},{8,10},{10,8},{9,1... | collective-permute-start | bytes 688136 | tf_op jit(solution)/shard_map/ppermute | solution.py:457
  17.0 1.8 %collective-permute-start.5 = (f32[6,8,8,128]{3,2,1,0:T(8,128)}, f32[6,8,8,128]{3,2,1,0:T(8,128)S(1)}, u32[]{:S(2)}, u32[]{:S(2)}) collective-permute-start(f32[6,8,8,128]{3,2,1,0:T(8,128)} %get-tuple-element.23), channel_id=1, source_target_pairs={{0,2},{2,0},{1,3},{3,1},{4,6},{6,4},{5,7},{7,5},{8,10},{10,8},{9,1... | collective-permute-start | bytes 589832 | tf_op jit(solution)/shard_map/ppermute | solution.py:457
  17.0 1.7 %collective-permute-start.10 = (f32[6,16,128]{2,1,0:T(8,128)S(1)}, f32[6,16,128]{2,1,0:T(8,128)S(1)}, u32[]{:S(2)}, u32[]{:S(2)}) collective-permute-start(f32[6,16,128]{2,1,0:T(8,128)S(1)} %collective-permute-done.4.refs_12_), channel_id=1, source_target_pairs={{0,2},{2,0},{1,3},{3,1},{4,6},{6,4},{5,7},{7,5},{8,10},{10,8},{9,1... | collective-permute-start | bytes 147464 | tf_op jit(solution)/shard_map/ppermute | solution.py:457
  17.6 1.3 %collective-permute-start.8 = (f32[8,16,128]{2,1,0:T(8,128)S(1)}, f32[8,16,128]{2,1,0:T(8,128)S(1)}, u32[]{:S(2)}, u32[]{:S(2)}) collective-permute-start(f32[8,16,128]{2,1,0:T(8,128)S(1)} %collective-permute-done.2.refs_10_), channel_id=1, source_target_pairs={{0,2},{2,0},{1,3},{3,1},{4,6},{6,4},{5,7},{7,5},{8,10},{10,8},{9,1... | collective-permute-start | bytes 196616 | tf_op jit(solution)/shard_map/ppermute | solution.py:457
  18.9 0.8 %copy-start.4 = (f32[8,16,128]{2,1,0:T(8,128)S(1)}, f32[8,16,128]{2,1,0:T(8,128)}, u32[]{:S(2)}) copy-start(f32[8,16,128]{2,1,0:T(8,128)} %get-tuple-element.15.refs_3_) | copy-start | bytes 196612
  19.8 0.8 %copy-start.5 = (f32[8,16,128]{2,1,0:T(8,128)S(1)}, f32[8,16,128]{2,1,0:T(8,128)}, u32[]{:S(2)}) copy-start(f32[8,16,128]{2,1,0:T(8,128)} %get-tuple-element.16.refs_4_) | copy-start | bytes 196612
  20.6 0.8 %copy-start.6 = (f32[8,16,128]{2,1,0:T(8,128)S(1)}, f32[8,16,128]{2,1,0:T(8,128)}, u32[]{:S(2)}) copy-start(f32[8,16,128]{2,1,0:T(8,128)} %get-tuple-element.17.refs_6_) | copy-start | bytes 196612
  55.7 0.7 %copy-start.8 = (f32[16]{0:T(128)S(1)}, f32[16]{0:T(128)}, u32[]{:S(2)}) copy-start(f32[16]{0:T(128)} %cond.1) | copy-start | bytes 196

commit v2 on v1

v2 whole, which is shorter than its diff:
```python
import functools
import math

import jax
import jax.numpy as jnp
from jax import lax
from jax.experimental import pallas as pl
from jax.experimental.pallas import tpu as pltpu
from jax.sharding import PartitionSpec as P

WINDOW_STEPS = 3
HALO = 2 * WINDOW_STEPS
LANES = 128
TILE = 8

step_size = 0.1
tau_inward = 0.3
tau_outward = 6.0
tau_opening = 12.0
tau_closing = 15.0
gate_level = 0.13
gate_width = 0.02
gradient_gain = 30.0
PAIR_OFFSETS = (
    (1, 0, 0),
    (0, 1, 0),
    (0, 0, 1),
    (1, 1, 0),
    (1, -1, 0),
    (1, 0, 1),
    (1, 0, -1),
    (0, 1, 1),
    (0, 1, -1),
)
DIRS = len(PAIR_OFFSETS)
Z_DIRS = tuple(d for d, o in enumerate(PAIR_OFFSETS) if o[2])
Y_DIRS = tuple(d for d, o in enumerate(PAIR_OFFSETS) if o[1])
V, G, S, H, B, A = range(6)
WIDTHS = (HALO, HALO, HALO, HALO - 1, WINDOW_STEPS, WINDOW_STEPS - 1)
STARTS = tuple(sum(WIDTHS[:f]) for f in range(6))
PLANES = sum(WIDTHS)
SLOT = 16


def matchings(count):
    result = []
    for parity in range(0 if count == 1 else 1 if count == 2 else 2):
        partner = [i + 1 if i % 2 == parity else i - 1 for i in range(count)]
        result.append([j if 0 <= j < count else None for j in partner])
    return result


def exchange(array, sizes, along_x=None, along_z=None):
    size_x, size_y, size_z = sizes
    pairs = []
    for i in range(size_x):
        for j in range(size_y):
            for k in range(size_z):
                x = along_x[i] if along_x else i
                z = along_z[k] if along_z else k
                to = (i, 1 - j, k) if x is None or z is None else (x, j, z)
                flat = [(p * size_y + q) * size_z + r for p, q, r in ((i, j, k), to)]
                pairs.append(tuple(flat))
    return lax.ppermute(array, ("gx", "gy", "gz"), pairs)


def looks_up(axis, parity):
    return lax.rem(lax.axis_index(axis), 2) == parity


def lane_ids(rows):
    return lax.broadcasted_iota(jnp.int32, (rows, LANES), 1)


def aligned(start):
    return start if isinstance(start, int) else pl.multiple_of(start, TILE)


def pack_kernel(nx, *refs):
    sources, outs, scratch = refs[:9], refs[9:-10], refs[-10:]
    sx, sz, sd = outs[:nx], outs[nx], outs[nx + 1 : 2 * nx + 1]
    sy, g_out, s_out, b_out = outs[2 * nx + 1 :]
    pot, gat, adh, reg, adv, rec, mask, sec, cond, landed = scratch
    copies = [
        pltpu.make_async_copy(source, place, landed.at[i])
        for i, (source, place) in enumerate(
            zip(sources, (pot, gat, adv, adh, rec, mask, sec, reg, cond), strict=True)
        )
    ]
    for i in (8, 5, 7, 6, 2, 4, 0, 1, 3):
        copies[i].start()
    X, Y, _ = pot.shape
    core = lax.axis_index("gy")
    for i in (8, 5, 7):
        copies[i].wait()
    label = reg[...]
    factor = jnp.zeros(label.shape, jnp.float32)
    for r in range(cond.shape[0]):
        factor = jnp.where(label == r, cond[r], factor)
    m = mask[...].astype(jnp.float32)
    g_out[...] = m * factor
    copies[6].wait()
    s_out[...] = sec[...].astype(jnp.float32)
    copies[2].wait()
    copies[4].wait()
    b_out[...] = adv[...] - m * rec[...]
    for i in (0, 1, 3):
        copies[i].wait()
    fields = (pot, g_out, s_out, gat, b_out, adh)
    for k in range(nx):
        up = looks_up("gx", k)
        for f, w in enumerate(WIDTHS):
            start = jnp.where(up, X - w, 0)
            sx[k][STARTS[f] : STARTS[f] + w] = fields[f][pl.ds(start, w)]
    lanes = lane_ids(X * Y)
    packed = pot[...].reshape(X * Y, LANES)
    for f in range(1, 6):
        rolled = pltpu.roll(fields[f][...].reshape(X * Y, LANES), SLOT * f, 1)
        inside = (lanes >= SLOT * f - SLOT // 2) & (lanes < SLOT * f + SLOT // 2)
        packed = jnp.where(inside, rolled, packed)
    sz[...] = packed.reshape(X, Y, LANES)
    for k in range(nx):
        start = jnp.where(looks_up("gx", k), X - HALO, 0)
        sd[k][...] = sz[pl.ds(start, HALO)]
    row = pl.multiple_of(jnp.where(core == 0, Y - TILE, 0), TILE)
    for f in range(6):
        sy[f] = fields[f][:, pl.ds(row, TILE), :]


def z_up(a, h):
    last = lane_ids(a.shape[0]) == LANES - 1
    ra, rh = pltpu.roll(a, LANES - 1, 1), pltpu.roll(h, LANES - 1, 1)
    return jnp.where(last, rh, ra), jnp.where(last, ra, rh)


def z_down(a, h):
    first = lane_ids(a.shape[0]) == 0
    ra, rh = pltpu.roll(a, 1, 1), pltpu.roll(h, 1, 1)
    return jnp.where(first, rh, ra), jnp.where(first, ra, rh)


def window_kernel(nx, nz, sizes, *refs):
    size_x, size_z = sizes
    it = iter(refs)

    def take(n):
        return [next(it) for _ in range(n)]

    tab, reg = take(2)
    own = take(6)
    rx, rz, rd = take(nx), take(nz), take(nx * nz)
    (yo,) = take(1)
    yx, yz, yd = take(nx), take(nz), take(nx * nz)
    out_v, out_h, out_t = take(3)
    U, MU = take(WINDOW_STEPS), take(WINDOW_STEPS)
    MK, FL, FZ, K, KZ = take(5)
    EH, SG = take(WINDOW_STEPS), take(WINDOW_STEPS)
    EG, ES, EB, EA, AV, AH, D, Q, RS = take(9)

    X, Y, _ = own[V].shape
    XE, YE = X + 2 * HALO, Y + TILE
    ROW = YE + TILE
    core = lax.axis_index("gy")
    xi, zi = lax.axis_index("gx"), lax.axis_index("gz")
    ro = pl.multiple_of(TILE * core, TILE)
    po = pl.multiple_of(Y * (1 - core), TILE)
    ps = pl.multiple_of((Y - TILE) * core, TILE)

    def at(x, row=0):
        return aligned(x * ROW + TILE + row)

    def load(ref, index, x, dy=0, rows=None, row=0):
        start = x * ROW + TILE + row + dy
        if not dy:
            start = aligned(start)
        return ref[index + (pl.ds(start, rows or YE), slice(None))]

    blank = jnp.zeros((TILE, LANES), jnp.float32)

    @pl.loop(0, XE + 1)
    def _(x):
        row = pl.multiple_of(x * ROW, TILE)
        for part in range(2):
            for kind in range(3):
                for n in range(WINDOW_STEPS):
                    U[n][kind, part, pl.ds(row, TILE), :] = blank
                    MU[n][kind, part, pl.ds(row, TILE), :] = blank
                MK[kind, part, pl.ds(row, TILE), :] = blank
            for d in Y_DIRS:
                K[d, part, pl.ds(row, TILE), :] = blank
                FL[d, part, pl.ds(row, TILE), :] = blank
            for i, d in enumerate(Z_DIRS):
                if d in Y_DIRS:
                    KZ[i, part, pl.ds(row, TILE), :] = blank
                    FZ[i, part, pl.ds(row, TILE), :] = blank

    stores = {G: EG, S: ES, H: EH[0], B: EB, A: EA}

    def put(f, part, xe, row, value):
        rows = value.shape[0]
        if f == V:
            U[0][0, part, pl.ds(at(xe, row), rows), :] = value
        else:
            stores[f][part, xe, pl.ds(row, rows), :] = value

    def spread(f, packs):
        parts = [pltpu.roll(p, (LANES - SLOT * f) % LANES, 1) if f else p for p in packs]
        if len(parts) == 1:
            value = parts[0]
        else:
            value = jnp.where(lane_ids(parts[0].shape[0]) < LANES // 2, *[
                jnp.where(looks_up("gz", 0), parts[0], parts[1]),
                jnp.where(looks_up("gz", 0), parts[1], parts[0]),
            ])
        return value

    def lanes_ok(rows):
        lanes = lane_ids(rows)
        right = (lanes < HALO) & (zi < size_z - 1)
        left = (lanes >= LANES - HALO) & (zi > 0)
        return right | left

    if nx < 2 or nz < 1:
        for ref in stores.values():
            ref[...] = jnp.zeros(ref.shape, jnp.float32)
        U[0][0] = jnp.zeros(U[0].shape[1:], jnp.float32)

    for f, w in enumerate(WIDTHS):
        for i in range(X):
            put(f, 0, HALO + i, ro, own[f][i])
            put(f, 0, HALO + i, po, yo[f, i])
        for k in range(nx):
            up = looks_up("gx", k)
            ok = jnp.where(up, xi < size_x - 1, xi > 0)
            dest = jnp.where(up, HALO + X, HALO - w)
            for i in range(w):
                mine = rx[k][STARTS[f] + i]
                theirs = yx[k][STARTS[f] + i, pl.ds(ps, TILE), :]
                if f == G:
                    mine, theirs = jnp.where(ok, mine, 0.0), jnp.where(ok, theirs, 0.0)
                put(f, 0, dest + i, ro, mine)
                put(f, 0, dest + i, po, theirs)

    if nz:

        def halo_plane(xe, ok, mine, theirs):
            for f in range(6):
                a, b = spread(f, mine), spread(f, theirs)
                if f == G:
                    a = jnp.where(lanes_ok(Y) & ok, a, 0.0)
                    b = jnp.where(lanes_ok(TILE) & ok, b, 0.0)
                put(f, 1, xe, ro, a)
                put(f, 1, xe, po, b)

        @pl.loop(0, X)
        def _(i):
            halo_plane(
                HALO + i, True, [r[i] for r in rz], [r[i, pl.ds(ps, TILE), :] for r in yz]
            )

        @pl.loop(0, HALO)
        def _(i):
            for k in range(nx):
                up = looks_up("gx", k)
                ok = jnp.where(up, xi < size_x - 1, xi > 0)
                dest = jnp.where(up, HALO + X, 0)
                halo_plane(
                    dest + i,
                    ok,
                    [r[i] for r in rd[k * nz : (k + 1) * nz]],
                    [r[i, pl.ds(ps, TILE), :] for r in yd[k * nz : (k + 1) * nz]],
                )

    def put_kinds(ref, index, x, a, h):
        rows = pl.ds(at(x), YE)
        for kind, (p, q) in enumerate(((a, h), z_up(a, h), z_down(a, h))):
            ref[index + (kind, 0, rows, slice(None))] = p
            ref[index + (kind, 1, rows, slice(None))] = q

    @pl.loop(0, XE)
    def _(x):
        rows = pl.ds(at(x), YE)
        v = [load(U[0], (0, part), x) for part in range(2)]
        for kind, pair in ((1, z_up(*v)), (2, z_down(*v))):
            for part in range(2):
                U[0][kind, part, rows, :] = pair[part]
        g = [EG[part, x] for part in range(2)]
        put_kinds(MK, (), x, *[jnp.where(t > 0.0, 1.0, 0.0) for t in g])
        sector = [
            jnp.where(g[part] > 0.0, ES[part, x], 0.0).astype(jnp.int32) for part in range(2)
        ]
        lines = [jnp.broadcast_to(tab[d : d + 1, :], (TILE, LANES)) for d in range(DIRS)]
        for t in range(0, YE, TILE):
            tile = pl.ds(at(x, t), TILE)
            flux = []
            for part in range(2):
                index = sector[part][t : t + TILE]
                flux.append(
                    [
                        g[part][t : t + TILE] * jnp.take_along_axis(line, index, axis=1)
                        for line in lines
                    ]
                )
                for d in range(DIRS):
                    FL[d, part, tile, :] = flux[part][d]
            for i, d in enumerate(Z_DIRS):
                dz = PAIR_OFFSETS[d][2]
                pair = (z_up if dz > 0 else z_down)(flux[0][d], flux[1][d])
                for part in range(2):
                    FZ[i, part, tile, :] = pair[part]

    def kind_of(dz):
        return 0 if dz == 0 else 1 if dz > 0 else 2

    @pl.loop(0, XE - 1)
    def _(x):
        rows = pl.ds(at(x), YE)
        for d, (dx, dy, dz) in enumerate(PAIR_OFFSETS):
            pair = []
            for part in range(2):
                there = (
                    load(FZ, (Z_DIRS.index(d), part), x + dx, dy)
                    if dz
                    else load(FL, (d, part), x + dx, dy)
                )
                pair.append(
                    load(FL, (d, part), x) * load(MK, (kind_of(dz), part), x + dx, dy)
                    + there * load(MK, (0, part), x)
                )
                K[d, part, rows, :] = pair[part]
            if dz:
                back = (z_down if dz > 0 else z_up)(*pair)
                for part in range(2):
                    KZ[Z_DIRS.index(d), part, rows, :] = back[part]

    def spread_of(u, x, part, rows=None, row=0, fill=False):
        total, couplings = None, None
        for d, (dx, dy, dz) in enumerate(PAIR_OFFSETS):
            for sign in (1, -1):
                if sign > 0:
                    coupling = load(K, (d, part), x, 0, rows, row)
                else:
                    ref, i = (KZ, Z_DIRS.index(d)) if dz else (K, d)
                    coupling = load(ref, (i, part), x - dx, -dy, rows, row)
                term = coupling * load(
                    u, (kind_of(sign * dz), part), x + sign * dx, sign * dy, rows, row
                )
                total = term if total is None else total + term
                if fill:
                    couplings = coupling if couplings is None else couplings + coupling
        here = pl.ds(row, rows or YE)
        if fill:
            D[part, x, here, :] = couplings
        else:
            couplings = D[part, x, here, :]
        centre = load(u, (0, part), x, 0, rows, row)
        return centre, total - couplings * centre

    for n in range(WINDOW_STEPS):
        reach = HALO - 1 - n
        last = n == WINDOW_STEPS - 1

        @pl.loop(HALO - reach, HALO + X + reach, unroll=2)
        def _(x, n=n, last=last):
            fresh = []
            for part in range(2):
                v, flow = spread_of(U[n], x, part, fill=n == 0)
                h = EH[n][part, x]
                s = jax.nn.sigmoid((v - gate_level) * (1.0 / gate_width))
                SG[n][part, x] = s
                rise = (step_size / tau_inward) * (v * v) * (1.0 - v)
                v_new = (v * (1.0 - step_size / tau_outward) + h * rise) + flow
                if last:
                    m = load(MK, (0, part), x)
                    a = EB[part, x] + m * v_new
                    AV[part, x] = a
                    fresh.append(m * a)
                else:
                    rest = s - 1.0
                    EH[n + 1][part, x] = h + (
                        rest * (h - 1.0) * (step_size / tau_opening)
                        - s * h * (step_size / tau_closing)
                    )
                    fresh.append(v_new)
            if last:
                put_kinds(MU[n], (), x, *fresh)
            else:
                put_kinds(U[n + 1], (), x, *fresh)

    def terms():
        row = ro

        @pl.loop(0, X)
        def _(i):
            x = HALO + i
            mu = [load(MU[n], (0, 0), x, 0, Y, row) for n in range(WINDOW_STEPS)]
            v = [load(U[n], (0, 0), x, 0, Y, row) for n in range(WINDOW_STEPS)]
            total = jnp.zeros((Y, LANES), jnp.float32)
            for d, (dx, dy, dz) in enumerate(PAIR_OFFSETS):
                edge = None
                for sign in (1, -1):
                    index = (kind_of(sign * dz), 0)
                    where = (x + sign * dx, sign * dy, Y, row)
                    part = None
                    for n in range(WINDOW_STEPS):
                        term = (load(MU[n], index, *where) - mu[n]) * (
                            load(U[n], index, *where) - v[n]
                        )
                        part = term if part is None else part + term
                    part = part * load(MK, index, *where)
                    edge = part if edge is None else edge + part
                total = total + load(FL, (d, 0), x, 0, Y, row) * edge
            Q[i] = total

        RS[...] = jnp.zeros(RS.shape, jnp.float32)
        label = reg[...]
        for r in range(SLOT):
            found = jnp.where(label == r, Q[...], 0.0)
            RS[r : r + 1, :] = jnp.sum(jnp.sum(found, axis=0), axis=0, keepdims=True)
        sums = lax.dot_general(
            jnp.ones((TILE, LANES), jnp.float32),
            RS[...],
            (((1,), (1,)), ((), ())),
            precision=lax.Precision.HIGHEST,
            preferred_element_type=jnp.float32,
        )
        sums = sums * jnp.broadcast_to(tab[DIRS : DIRS + 1, :], sums.shape)
        for i in range(0, out_t.shape[0], TILE):
            out_t[i : i + TILE] = sums

    for n in reversed(range(WINDOW_STEPS)):
        if n == 0:
            terms()
        first, final = n == WINDOW_STEPS - 1, n == 0

        @pl.loop(HALO - n, HALO + X + n, unroll=2)
        def _(x, n=n, first=first, final=final):
            fresh = []
            for part in range(1 if final else 2):
                rows, row = (Y, ro) if final else (YE, 0)
                here = pl.ds(row, rows)
                m = load(MK, (0, part), x, 0, rows, row)
                v = load(U[n], (0, part), x, 0, rows, row)
                h = EH[n][part, x, here, :]
                s = SG[n][part, x, here, :]
                a = AV[part, x, here, :]
                e = EA[part, x, here, :] if first else AH[part, x, here, :]
                _, flow = spread_of(MU[n], x, part, rows, row)
                in_v = v * (step_size / tau_inward)
                f_v = h * in_v * (2.0 - 3.0 * v) - step_size / tau_outward
                f_h = in_v * v * (1.0 - v)
                open_, close = step_size / tau_opening, step_size / tau_closing
                g_v = s * (1.0 - s) * (
                    h * ((open_ - close) / gate_width) - open_ / gate_width
                )
                g_h = s * (open_ - close) - open_
                a_new = (a + flow) + m * (f_v * a + g_v * e)
                e_new = e + m * (f_h * a + g_h * e)
                if final:
                    out_v[x - HALO] = a_new
                    out_h[x - HALO] = e_new
                else:
                    AV[part, x] = a_new
                    AH[part, x] = e_new
                    fresh.append(m * a_new)
            if not final:
                put_kinds(MU[n - 1], (), x, *fresh)


def vmem(n):
    return [pl.BlockSpec(memory_space=pltpu.VMEM)] * n


def local(pot, gat, adv, adh, rec, mask, sec, reg, table, cond):
    X, Y, Z = pot.shape
    size_x, size_y, size_z = (lax.axis_size(a) for a in ("gx", "gy", "gz"))
    assert size_y == 2 and Z == LANES and X >= HALO and Y % TILE == 0 and Y >= TILE
    assert table.shape[0] <= LANES and cond.shape[0] <= SLOT
    mx, mz = matchings(size_x), matchings(size_z)
    nx, nz = len(mx), len(mz)
    f32 = jnp.float32
    block = jax.ShapeDtypeStruct((X, Y, Z), f32)
    whole = pltpu.VMEM((X, Y, Z), f32)
    args = (pot, gat, adv, adh, rec, mask, sec, reg, cond)
    ints = pltpu.VMEM((X, Y, Z), jnp.int32)
    packed = pl.pallas_call(
        functools.partial(pack_kernel, nx),
        out_shape=[jax.ShapeDtypeStruct((PLANES, Y, Z), f32)] * nx
        + [block]
        + [jax.ShapeDtypeStruct((HALO, Y, Z), f32)] * nx
        + [jax.ShapeDtypeStruct((6, X, TILE, Z), f32)]
        + [block] * 3,
        in_specs=[pl.BlockSpec(memory_space=pltpu.HBM)] * 9,
        out_specs=vmem(2 * nx + 5),
        scratch_shapes=[whole, whole, whole, ints, whole, whole, ints, ints,
            pltpu.SMEM(cond.shape, f32),
            pltpu.SemaphoreType.DMA((9,))],
        compiler_params=pltpu.CompilerParams(vmem_limit_bytes=8 << 20),
        name="pack",
    )(*[pltpu.with_memory_space_constraint(a, pltpu.HBM) for a in args])
    sx, sz, sd = packed[:nx], packed[nx], packed[nx + 1 : 2 * nx + 1]
    sy, g, s, b = packed[2 * nx + 1 :]

    sizes = (size_x, size_y, size_z)
    rx = [exchange(sx[k], sizes, mx[k]) for k in range(nx)]
    rz = [exchange(sz, sizes, None, mz[k]) for k in range(nz)]
    rd = [exchange(sd[i], sizes, mx[i], mz[k]) for i in range(nx) for k in range(nz)]
    swap = [(0, 1), (1, 0)]
    over = lambda arrays: [lax.ppermute(a, "gy", swap) for a in arrays]
    (yo,) = over([sy])
    yx, yz, yd = over(rx), over(rz), over(rd)

    cells = X * Y * Z * size_x * size_y * size_z
    scale = gradient_gain / math.sqrt(cells / cond.shape[0])
    tab = jnp.concatenate(
        [
            jnp.pad(0.5 * table.T, ((0, 0), (0, LANES - table.shape[0]))),
            jnp.pad((-scale / cond)[None], ((0, 0), (0, LANES - cond.shape[0]))),
            jnp.zeros((SLOT - DIRS - 1, LANES), f32),
        ]
    )
    devices = size_x * size_y * size_z
    XE, YE = X + 2 * HALO, Y + TILE
    rows = XE * (YE + TILE) + 2 * TILE
    pad = lambda *lead: pltpu.VMEM(lead + (2, rows, LANES), f32)
    ext = lambda *lead: pltpu.VMEM(lead + (2, XE, YE, LANES), f32)
    steps = WINDOW_STEPS
    operands = [tab, reg, pot, g, s, gat, b, adh, *rx, *rz, *rd, yo, *yx, *yz, *yd]
    lam_v, lam_h, tot = pl.pallas_call(
        functools.partial(window_kernel, nx, nz, (size_x, size_z)),
        out_shape=[block, block, jax.ShapeDtypeStruct((devices, LANES), f32)],
        in_specs=vmem(len(operands)),
        out_specs=vmem(3),
        scratch_shapes=[
            *[pad(3)] * (2 * steps),
            pad(3), pad(DIRS), pad(len(Z_DIRS)), pad(DIRS), pad(len(Z_DIRS)),
            *[ext()] * (2 * steps + 7),
            pltpu.VMEM((X, Y, LANES), f32), pltpu.VMEM((LANES, LANES), f32),
        ],
        compiler_params=pltpu.CompilerParams(vmem_limit_bytes=42 << 20),
        name="window",
    )(*operands)
    every = lax.all_to_all(tot.reshape(devices, 1, LANES), ("gx", "gy", "gz"), 0, 0)
    return lam_v, lam_h, jnp.sum(every, axis=(0, 1))[: cond.shape[0]]


def solution(mesh):
    cells = P(("twin", "gx"), "gy", "gz")
    in_specs = (cells,) * 8 + (P("twin", None), P("twin"))
    out_specs = (cells, cells, P("twin"))
    return jax.shard_map(local, mesh=mesh, in_specs=in_specs, out_specs=out_specs, check_vma=False)
```

time: 57.3 us -> 46.7 us (0.82)
  Pallas kernels: 26.3 us -> 20.6 us
  local copies, waits for them, and re-layouts: 3.25 us -> 0.2 us
  starting transfers between devices: 12.3 us -> 9.28 us
  blocking collectives: 10.2 us -> 10.9 us
  waiting for transfers between devices: 3.52 us -> 4.11 us
    pallas_call x1, Pallas kernels: 24.1 us -> 19.2 us  [local(): pl.pallas_call(functools.partial(window_kernel, nx, nz, (size_x, size_z))...]
    ppermute x5, starting transfers between devices: 11.2 us -> 7.73 us  [exchange(): return lax.ppermute(array, ('gx', 'gy', 'gz'), pairs)]
    unnamed x19 -> x13, local copies, waits for them, and re-layouts: 3.25 us -> 0.12 us
    ppermute x5, waiting for transfers between devices: 2.3 us -> 3.27 us  [exchange(): return lax.ppermute(array, ('gx', 'gy', 'gz'), pairs)]
    pallas_call x1, Pallas kernels: 2.19 us -> 1.38 us  [local(): pl.pallas_call(functools.partial(pack_kernel, nx), out_shape=[jax.ShapeDt...]
    all_to_all x1, blocking collectives: 10.2 us -> 10.9 us  [local(): lax.all_to_all(tot.reshape(devices, 1, LANES), ('gx', 'gy', 'gz'), 0, 0)]
  transfers between devices with their start and end apart: 11 -> 11, of which waited for: 4 -> 4; matrix products, arithmetic and copies ran while one was open for 0% -> 1% of each run, Pallas kernels for 0% -> 0%
where the time goes in v2:
time: 46.7 us; the launch traced here: 46.5 us
  Pallas kernels  20.6 us (44%)
  blocking collectives  10.9 us (23%)
  starting transfers between devices  9.28 us (20%)
  waiting for transfers between devices  4.11 us (9%)
  between operations  0.74 us (2%)
  other arithmetic  0.63 us (1%)
    pallas_call x1, Pallas kernels, local(): pl.pallas_call(functools.partial(window_kernel, nx, nz, (size_x, size_z))...  19.2 us
    all_to_all x1, blocking collectives, local(): lax.all_to_all(tot.reshape(devices, 1, LANES), ('gx', 'gy', 'gz'), 0, 0)  10.9 us
    ppermute x5, starting transfers between devices, exchange(): return lax.ppermute(array, ('gx', 'gy', 'gz'), pairs)  7.73 us
    ppermute x5, waiting for transfers between devices, exchange(): return lax.ppermute(array, ('gx', 'gy', 'gz'), pairs)  3.27 us
    ppermute x6, starting transfers between devices, local(): over = lambda arrays: [lax.ppermute(a, 'gy', swap) for a in arrays]  1.54 us
    pallas_call x1, Pallas kernels, local(): pl.pallas_call(functools.partial(pack_kernel, nx), out_shape=[jax.ShapeDt...  1.38 us
  transfers between devices with their start and end apart: 11, of which 4 were waited for; matrix products, arithmetic and copies ran while one was open for 1% of the time, Pallas kernels for 0%

profile of v2, /device:TPU:0, one launch (start us, length us, event | category | flops | bytes accessed | tf_op | source)
XLA Modules:
  0.0 46.5 jit_solution(2304416900533242147)
XLA Ops:
  0.6 0.0 copy-start.4
  0.6 0.0 copy-start.5
  0.7 0.0 copy-start.1
  0.7 0.0 copy-start.2
  0.7 0.0 copy-start.3
  0.7 1.4 %pack.1 = (f32[28,16,128]{2,1,0:T(8,128)S(1)}, f32[28,16,128]{2,1,0:T(8,128)S(1)}, f32[8,16,128]{2,1,0:T(8,128)S(1)}, f32[6,16,128]{2,1,0:T(8,128)S(1)}, f32[6,1...) custom-call(f32[8,16,128]{2,1,0:T(8,128)} %refs_2_.3, ...), custom_call_target="tpu_custom_call" | custom-call | tf_op jit(solution)/shard_map/pack/pallas_call | solution.py:486
  2.1 0.0 copy-start
  2.1 3.1 %collective-permute-start = (f32[28,16,128]{2,1,0:T(8,128)S(1)}, f32[28,16,128]{2,1,0:T(8,128)S(1)}, u32[]{:S(2)}, u32[]{:S(2)}) collective-permute-start(f32[28,16,128]{2,1,0:T(8,128)S(1)} %get-tuple-element.18), channel_id=1, source_target_pairs={{0,4},{1,5},{2,6},{3,7},{4,0},{5,1},{6,2},{7,3},{8,12},{9,13},{10,... | collective-permute-start | bytes 688136 | tf_op jit(solution)/shard_map/ppermute | solution.py:64
  5.2 0.0 collective-permute-start.1
  5.2 4.1 %collective-permute-start.3 = (f32[6,16,128]{2,1,0:T(8,128)S(1)}, f32[6,16,128]{2,1,0:T(8,128)S(1)}, u32[]{:S(2)}, u32[]{:S(2)}) collective-permute-start(f32[6,16,128]{2,1,0:T(8,128)S(1)} %get-tuple-element.21), channel_id=1, source_target_pairs={{0,5},{1,4},{2,7},{3,6},{4,1},{5,0},{6,3},{7,2},{8,13},{9,12},{10,... | collective-permute-start | bytes 147464 | tf_op jit(solution)/shard_map/ppermute | solution.py:64
  9.3 0.0 collective-permute-start.4
  9.3 0.5 %collective-permute-start.2 = (f32[8,16,128]{2,1,0:T(8,128)S(1)}, f32[8,16,128]{2,1,0:T(8,128)S(1)}, u32[]{:S(2)}, u32[]{:S(2)}) collective-permute-start(f32[8,16,128]{2,1,0:T(8,128)S(1)} %get-tuple-element.20), channel_id=1, source_target_pairs={{0,1},{1,0},{2,3},{3,2},{4,5},{5,4},{6,7},{7,6},{8,9},{9,8},{10,11... | collective-permute-start | bytes 196616 | tf_op jit(solution)/shard_map/ppermute | solution.py:64
  9.8 0.0 copy-done.4
  9.8 0.1 copy.14
  9.9 3.1 %collective-permute-done.3.refs_11_ = f32[6,16,128]{2,1,0:T(8,128)S(1)} collective-permute-done((f32[6,16,128]{2,1,0:T(8,128)S(1)}, f32[6,16,128]{2,1,0:T(8,128)S(1)}, u32[]{:S(2)}, u32[]{:S(2)}) %collective-permute-start.3) | collective-permute-done | bytes 49184 | tf_op jit(solution)/shard_map/ppermute | solution.py:64
  13.1 0.0 collective-permute-start.9
  13.1 0.0 collective-permute-done.refs_8_
  13.1 0.5 %collective-permute-start.6 = (f32[28,16,128]{2,1,0:T(8,128)S(1)}, f32[28,16,128]{2,1,0:T(8,128)S(1)}, u32[]{:S(2)}, u32[]{:S(2)}) collective-permute-start(f32[28,16,128]{2,1,0:T(8,128)S(1)} %collective-permute-done.refs_8_), channel_id=1, source_target_pairs={{0,2},{2,0},{1,3},{3,1},{4,6},{6,4},{5,7},{7,5},{8,10},{10,8},{9,1... | collective-permute-start | bytes 688136 | tf_op jit(solution)/shard_map/ppermute | solution.py:509
  13.6 0.0 collective-permute-done.1.refs_9_
  13.6 0.1 collective-permute-start.7
  13.6 0.0 copy-done.5
  13.7 0.1 pad.12.clone
  13.7 0.0 collective-permute-done.4.refs_12_
  13.7 0.5 collective-permute-start.5
  14.2 0.1 collective-permute-done.2.refs_10_
  14.3 0.0 collective-permute-start.10
  14.3 0.0 collective-permute-done.9.refs_17_
  14.3 0.5 %collective-permute-start.8 = (f32[8,16,128]{2,1,0:T(8,128)S(1)}, f32[8,16,128]{2,1,0:T(8,128)S(1)}, u32[]{:S(2)}, u32[]{:S(2)}) collective-permute-start(f32[8,16,128]{2,1,0:T(8,128)S(1)} %collective-permute-done.2.refs_10_), channel_id=1, source_target_pairs={{0,2},{2,0},{1,3},{3,1},{4,6},{6,4},{5,7},{7,5},{8,10},{10,8},{9,1... | collective-permute-start | bytes 196616 | tf_op jit(solution)/shard_map/ppermute | solution.py:509
  14.8 0.1 fusion.refs_0_
  14.9 0.6 %collective-permute-done.10.refs_18_ = f32[6,16,128]{2,1,0:T(8,128)S(1)} collective-permute-done((f32[6,16,128]{2,1,0:T(8,128)S(1)}, f32[6,16,128]{2,1,0:T(8,128)S(1)}, u32[]{:S(2)}, u32[]{:S(2)}) %collective-permute-start.10) | collective-permute-done | bytes 49184 | tf_op jit(solution)/shard_map/ppermute | solution.py:509
  15.6 0.2 collective-permute-done.8.refs_16_
  15.7 0.0 collective-permute-done.5.refs_13_
  15.7 0.0 collective-permute-done.6.refs_14_
  15.7 0.0 collective-permute-done.7.refs_15_
  15.7 0.0 copy-done.1
  15.8 0.0 copy-done.2
  15.8 0.0 copy-done.3
  15.8 0.0 copy-done
  15.8 19.2 %window.1 = (f32[8,16,128]{2,1,0:T(8,128)}, f32[8,16,128]{2,1,0:T(8,128)}, f32[16,128]{1,0:T(8,128)S(1)}) custom-call(f32[16,128]{1,0:T(8,128)S(1)} %fusion.refs_0_, s32[8,16,128]{2,1,0:T(8,128)S(1)} %copy-done, f32[8,16,128]{2,1,0:T(8,128)S(1)} %copy-done.1, f32[8,16,128]{2,1,0:T(8,128)S(1)} %get-tuple-element.15.refs_3_, ...), custom_call_target="tpu_custom_call" | custom-call | tf_op jit(solution)/shard_map/window/pallas_call | solution.py:529
  35.0 10.9 %all_to_all.5 = f32[16,1,128]{2,1,0:T(1,128)S(1)} all-to-all(f32[16,1,128]{2,1,0:T(1,128)S(1)} %bitcast.8), channel_id=1, replica_groups=mesh['twin'=2,'gx'=4,'gy'=2,'gz'=2] {'gx','gy','gz'}, dimensions={0} | all-to-all | bytes 16384 | tf_op jit(solution)/shard_map/all_to_all | solution.py:543
  46.0 0.5 %reduce_sum.9 = f32[128]{0:T(128)} reduce(f32[16,1,128]{2,1,0:T(1,128)S(1)} %all_to_all.5, f32[]{:T(128)} %constant.4.clone.1), dimensions={0,1}, to_apply=%region_0.1 | reduce | flops 1920 | bytes 8708 | tf_op jit(solution)/shard_map/reduce_sum | solution.py:544
  (3 shorter events, 0.0 us)
Async XLA Ops:
  0.6 9.2 %copy-start.4 = (f32[12,9]{1,0:T(8,128)S(1)}, f32[12,9]{1,0:T(8,128)}, u32[]{:S(2)}) copy-start(f32[12,9]{1,0:T(8,128)} %param.18) | copy-start | bytes 1300
  0.6 13.0 %copy-start.5 = (f32[16]{0:T(128)S(1)}, f32[16]{0:T(128)}, u32[]{:S(2)}) copy-start(f32[16]{0:T(128)} %refs_8_.1) | copy-start | bytes 196
  0.7 15.1 %copy-start.1 = (f32[8,16,128]{2,1,0:T(8,128)S(1)}, f32[8,16,128]{2,1,0:T(8,128)}, u32[]{:S(2)}) copy-start(f32[8,16,128]{2,1,0:T(8,128)} %refs_2_.3) | copy-start | bytes 196612
  0.7 15.1 %copy-start.2 = (f32[8,16,128]{2,1,0:T(8,128)S(1)}, f32[8,16,128]{2,1,0:T(8,128)}, u32[]{:S(2)}) copy-start(f32[8,16,128]{2,1,0:T(8,128)} %refs_5_.3) | copy-start | bytes 196612
  0.7 15.1 %copy-start.3 = (f32[8,16,128]{2,1,0:T(8,128)S(1)}, f32[8,16,128]{2,1,0:T(8,128)}, u32[]{:S(2)}) copy-start(f32[8,16,128]{2,1,0:T(8,128)} %refs_7_.3) | copy-start | bytes 196612
  2.1 13.7 %copy-start = (s32[8,16,128]{2,1,0:T(8,128)S(1)}, s32[8,16,128]{2,1,0:T(8,128)}, u32[]{:S(2)}) copy-start(s32[8,16,128]{2,1,0:T(8,128)} %refs_1_.3) | copy-start | bytes 196612
  2.1 11.0 %collective-permute-start = (f32[28,16,128]{2,1,0:T(8,128)S(1)}, f32[28,16,128]{2,1,0:T(8,128)S(1)}, u32[]{:S(2)}, u32[]{:S(2)}) collective-permute-start(f32[28,16,128]{2,1,0:T(8,128)S(1)} %get-tuple-element.18), channel_id=1, source_target_pairs={{0,4},{1,5},{2,6},{3,7},{4,0},{5,1},{6,2},{7,3},{8,12},{9,13},{10,... | collective-permute-start | bytes 688136 | tf_op jit(solution)/shard_map/ppermute | solution.py:64
  5.2 8.4 %collective-permute-start.1 = (f32[28,16,128]{2,1,0:T(8,128)S(1)}, f32[28,16,128]{2,1,0:T(8,128)S(1)}, u32[]{:S(2)}, u32[]{:S(2)}) collective-permute-start(f32[28,16,128]{2,1,0:T(8,128)S(1)} %get-tuple-element.19), channel_id=1, source_target_pairs={{0,2},{1,3},{2,0},{3,1},{4,8},{5,9},{6,10},{7,11},{8,4},{9,5},{10,... | collective-permute-start | bytes 688136 | tf_op jit(solution)/shard_map/ppermute | solution.py:64
  5.2 7.8 %collective-permute-start.3 = (f32[6,16,128]{2,1,0:T(8,128)S(1)}, f32[6,16,128]{2,1,0:T(8,128)S(1)}, u32[]{:S(2)}, u32[]{:S(2)}) collective-permute-start(f32[6,16,128]{2,1,0:T(8,128)S(1)} %get-tuple-element.21), channel_id=1, source_target_pairs={{0,5},{1,4},{2,7},{3,6},{4,1},{5,0},{6,3},{7,2},{8,13},{9,12},{10,... | collective-permute-start | bytes 147464 | tf_op jit(solution)/shard_map/ppermute | solution.py:64
  9.3 4.4 %collective-permute-start.4 = (f32[6,16,128]{2,1,0:T(8,128)S(1)}, f32[6,16,128]{2,1,0:T(8,128)S(1)}, u32[]{:S(2)}, u32[]{:S(2)}) collective-permute-start(f32[6,16,128]{2,1,0:T(8,128)S(1)} %get-tuple-element.22), channel_id=1, source_target_pairs={{0,2},{1,3},{2,0},{3,1},{4,9},{5,8},{6,11},{7,10},{8,5},{9,4},{10,... | collective-permute-start | bytes 147464 | tf_op jit(solution)/shard_map/ppermute | solution.py:64
  9.3 5.0 %collective-permute-start.2 = (f32[8,16,128]{2,1,0:T(8,128)S(1)}, f32[8,16,128]{2,1,0:T(8,128)S(1)}, u32[]{:S(2)}, u32[]{:S(2)}) collective-permute-start(f32[8,16,128]{2,1,0:T(8,128)S(1)} %get-tuple-element.20), channel_id=1, source_target_pairs={{0,1},{1,0},{2,3},{3,2},{4,5},{5,4},{6,7},{7,6},{8,9},{9,8},{10,11... | collective-permute-start | bytes 196616 | tf_op jit(solution)/shard_map/ppermute | solution.py:64
  13.1 1.3 %collective-permute-start.9 = (f32[6,16,128]{2,1,0:T(8,128)S(1)}, f32[6,16,128]{2,1,0:T(8,128)S(1)}, u32[]{:S(2)}, u32[]{:S(2)}) collective-permute-start(f32[6,16,128]{2,1,0:T(8,128)S(1)} %collective-permute-done.3.refs_11_), channel_id=1, source_target_pairs={{0,2},{2,0},{1,3},{3,1},{4,6},{6,4},{5,7},{7,5},{8,10},{10,8},{9,1... | collective-permute-start | bytes 147464 | tf_op jit(solution)/shard_map/ppermute | solution.py:509
  13.1 2.7 %collective-permute-start.6 = (f32[28,16,128]{2,1,0:T(8,128)S(1)}, f32[28,16,128]{2,1,0:T(8,128)S(1)}, u32[]{:S(2)}, u32[]{:S(2)}) collective-permute-start(f32[28,16,128]{2,1,0:T(8,128)S(1)} %collective-permute-done.refs_8_), channel_id=1, source_target_pairs={{0,2},{2,0},{1,3},{3,1},{4,6},{6,4},{5,7},{7,5},{8,10},{10,8},{9,1... | collective-permute-start | bytes 688136 | tf_op jit(solution)/shard_map/ppermute | solution.py:509
  13.6 2.2 %collective-permute-start.7 = (f32[28,16,128]{2,1,0:T(8,128)S(1)}, f32[28,16,128]{2,1,0:T(8,128)S(1)}, u32[]{:S(2)}, u32[]{:S(2)}) collective-permute-start(f32[28,16,128]{2,1,0:T(8,128)S(1)} %collective-permute-done.1.refs_9_), channel_id=1, source_target_pairs={{0,2},{2,0},{1,3},{3,1},{4,6},{6,4},{5,7},{7,5},{8,10},{10,8},{9,1... | collective-permute-start | bytes 688136 | tf_op jit(solution)/shard_map/ppermute | solution.py:509
  13.7 2.0 %collective-permute-start.5 = (f32[6,8,8,128]{3,2,1,0:T(8,128)S(1)}, f32[6,8,8,128]{3,2,1,0:T(8,128)S(1)}, u32[]{:S(2)}, u32[]{:S(2)}) collective-permute-start(f32[6,8,8,128]{3,2,1,0:T(8,128)S(1)} %get-tuple-element.23), channel_id=1, source_target_pairs={{0,2},{2,0},{1,3},{3,1},{4,6},{6,4},{5,7},{7,5},{8,10},{10,8},{9,1... | collective-permute-start | bytes 589832 | tf_op jit(solution)/shard_map/ppermute | solution.py:509
  14.3 1.2 %collective-permute-start.10 = (f32[6,16,128]{2,1,0:T(8,128)S(1)}, f32[6,16,128]{2,1,0:T(8,128)S(1)}, u32[]{:S(2)}, u32[]{:S(2)}) collective-permute-start(f32[6,16,128]{2,1,0:T(8,128)S(1)} %collective-permute-done.4.refs_12_), channel_id=1, source_target_pairs={{0,2},{2,0},{1,3},{3,1},{4,6},{6,4},{5,7},{7,5},{8,10},{10,8},{9,1... | collective-permute-start | bytes 147464 | tf_op jit(solution)/shard_map/ppermute | solution.py:509
  14.3 1.4 %collective-permute-start.8 = (f32[8,16,128]{2,1,0:T(8,128)S(1)}, f32[8,16,128]{2,1,0:T(8,128)S(1)}, u32[]{:S(2)}, u32[]{:S(2)}) collective-permute-start(f32[8,16,128]{2,1,0:T(8,128)S(1)} %collective-permute-done.2.refs_10_), channel_id=1, source_target_pairs={{0,2},{2,0},{1,3},{3,1},{4,6},{6,4},{5,7},{7,5},{8,10},{10,8},{9,1... | collective-permute-start | bytes 196616 | tf_op jit(solution)/shard_map/ppermute | solution.py:509
